TPU v7x, 256 devices: a whole 4x4x8 slice. The times are simulated.
256 devices in a mesh: seq: 32 (over x, z), head: 8 (over y, core).
Axes of the slice: x: 4, y: 4, z: 8, core: 2. Of those that a mesh axis runs over, the one named last changes fastest.
Arguments:
- layer_input: bfloat16 [8192, 4096], P('seq', 'head'), may hold values from -6 to 6
- value_weight: bfloat16 [4096, 4096], P(None, 'head'), may hold values from -0.09375 to 0.09375
- state_weight: bfloat16 [4096, 2048], P(None, 'head'), may hold values from -0.02734375 to 0.02734375
- output_weight: bfloat16 [4096, 4096], P('head'), may hold values from -0.09375 to 0.09375
- log_decay: float32 [64, 8192], P('head', 'seq'), may hold values from -1.5 to 0, as said below
- skip_gain: float32 [64], P('head'), may hold values from 0.5 to 1.5
- output_grad: bfloat16 [8192, 4096], P('seq', 'head'), may hold values from -6 to 6
Outputs:
- layer_output: bfloat16 [8192, 4096], P('seq', 'head')
- input_grad: bfloat16 [8192, 4096], P('seq', 'head')
Inputs may be any that keep to these rules, and one draw needn't show every extreme that they name: `log_decay`: each entry is below zero.
All inputs are finite; a program needn't handle non-finite values.
Results may differ from a plain program's by a relative error of at most 0.015.
Values may be sent and summed in bfloat16 or wider, within the bound.
No kernel may reach another device: no remote copies, remote signals or barrier semaphores. Data moves between devices by JAX's collectives and lax.ppermute only.
A program may use at most 64 MiB of HBM per device.

v0:
```python
import functools

import jax
import jax.numpy as jnp
from jax import lax
from jax.experimental import pallas as pl
from jax.experimental.pallas import tpu as pltpu
from jax.sharding import Mesh
from jax.sharding import PartitionSpec as P


STATE = 128
HEADS = 8
SEQ = ("x", "z")
F32 = jnp.float32
BF16 = jnp.bfloat16
NN = (((1,), (0,)), ((), ()))
NT = (((1,), (1,)), ((), ()))
TN = (((0,), (0,)), ((), ()))


def dot(a, b, dims):
    return lax.dot_general(a, b, dims, preferred_element_type=F32)


def spec(shape, kind=F32):
    return jax.ShapeDtypeStruct(shape, kind)


def call(body, outs, *args, flops=2**24, scratch=(), limit=24):
    moved = sum(a.size * a.dtype.itemsize for a in args)
    moved += sum(o.size * o.dtype.itemsize for o in outs)
    vmem = pl.BlockSpec(memory_space=pltpu.VMEM)
    return pl.pallas_call(
        body,
        out_shape=outs,
        in_specs=[vmem] * len(args),
        out_specs=[vmem] * len(outs),
        scratch_shapes=list(scratch),
        compiler_params=pltpu.CompilerParams(vmem_limit_bytes=limit * 2**20),
        cost_estimate=pl.CostEstimate(flops=flops, bytes_accessed=moved, transcendentals=0),
    )(*args)


def shift(array, axis, step):
    size = lax.axis_size(axis)
    return lax.ppermute(array, axis, [(i, (i + step) % size) for i in range(size)])


def parts_of(array):
    high = array.astype(BF16)
    rest = array - high.astype(F32)
    middle = rest.astype(BF16)
    return high, middle, (rest - middle.astype(F32)).astype(BF16)


def exact(parts, ones, dims, first):
    total = 0.0
    for part in parts:
        total = total + (dot(part, ones, dims) if first else dot(ones, part, dims))
    return total


def ones_where(keep):
    return jnp.where(keep, 1.0, 0.0).astype(BF16)


def iota(shape, dim):
    return lax.broadcasted_iota(jnp.int32, shape, dim)


def pair_lanes(array, two):
    shape = (array.shape[0], 128)
    low = jnp.broadcast_to(array[:, 2 * two : 2 * two + 1], shape)
    high = jnp.broadcast_to(array[:, 2 * two + 1 : 2 * two + 2], shape)
    return jnp.where(iota(shape, 1) < 64, low, high)


def inflow_of(decay):
    u = -2.0 * decay
    series = 1.0
    for k in (8, 7, 6, 5, 4, 3, 2):
        series = 1.0 - u * (1.0 / k) * series
    return jnp.sqrt(jnp.where(u < 0.5, u * series, 1.0 - jnp.exp(-u)))


def prepare_kernel(decay_ref, gain_ref, kernels, entering, to_end, totals, skip):
    decay = decay_ref[...]
    rows = decay.shape[1]
    square = (rows, rows)
    parts = parts_of(decay)
    row = exact(parts, ones_where(iota(square, 0) <= iota(square, 1)), NN, True)
    column = exact(parts, ones_where(iota(square, 1) <= iota(square, 0)), NT, False)
    decay_col = exact(parts, ones_where(iota(square, 1) == iota(square, 0)), NT, False)
    inflow_row = inflow_of(decay)
    causal = iota(square, 0) >= iota(square, 1)
    for h in range(HEADS):
        spread = jnp.where(causal, column[:, h : h + 1] - row[h : h + 1, :], -1e30)
        kernels[h] = (jnp.exp(spread) * inflow_row[h : h + 1, :]).astype(BF16)
    inflow_col = inflow_of(decay_col)
    total = column[rows - 1 : rows, :]
    total = jnp.broadcast_to(total, (8, HEADS))
    lanes = (HEADS, 128)
    spread = 0.0
    for k, part in enumerate(parts_of(total)):
        place = ones_where(iota(lanes, 1) == iota(lanes, 0) + HEADS * k)
        spread = spread + dot(part, place, NN)
    totals[...] = spread.astype(BF16)
    end = jnp.exp(total[0:1] - column) * inflow_col
    start = jnp.exp(column)
    for two in range(HEADS // 2):
        at = slice(two * 128, two * 128 + 128)
        entering[:, at] = pair_lanes(start, two)
        to_end[:, at] = pair_lanes(end, two)
        skip[:, at] = pair_lanes(gain_ref[...], two)


def weights_kernel(other, value_ref, state_ref, out_ref, value_to, state_to, out_to, sems):
    shard = value_to.shape[1]
    y, c = lax.axis_index("y"), lax.axis_index("c")
    core = 1 - c if other else c
    copies = []
    for k in range(4):
        at = pl.multiple_of((((y + k) % 4) * 2 + core) * shard, shard)
        copies.append((value_ref.at[pl.ds(at, shard), :], value_to.at[k]))
        copies.append((state_ref.at[pl.ds(at, shard), :], state_to.at[k]))
        copies.append((out_ref.at[:, pl.ds(at, shard)], out_to.at[k]))
    started = []
    for i, (source, target) in enumerate(copies):
        copy = pltpu.make_async_copy(source, target, sems.at[i])
        copy.start()
        started.append(copy)
    for copy in started:
        copy.wait()


def weights_of(other, value_weight, state_weight, output_weight, shard):
    width, pair = value_weight.shape[1], state_weight.shape[1]
    shapes = [(4, shard, width), (4, shard, pair), (4, width, shard)]
    return pl.pallas_call(
        functools.partial(weights_kernel, other),
        out_shape=[spec(s, BF16) for s in shapes],
        in_specs=[pl.BlockSpec(memory_space=pltpu.HBM)] * 3,
        out_specs=[pl.BlockSpec(memory_space=pltpu.VMEM)] * 3,
        scratch_shapes=[pltpu.SemaphoreType.DMA((12,))],
        compiler_params=pltpu.CompilerParams(vmem_limit_bytes=8 * 2**20),
        cost_estimate=pl.CostEstimate(flops=0, bytes_accessed=10 * 2**20, transcendentals=0),
    )(*[pltpu.with_memory_space_constraint(w, pltpu.HBM) for w in (value_weight, state_weight, output_weight)])


def input_first(
    own, low, high, value_a, state_a, value_b, state_b, own_ref, other_ref
):
    for value, state, out in ((value_b, state_b, other_ref), (value_a, state_a, own_ref)):
        width = value.shape[2]
        for weight, at in ((value, slice(0, width)), (state, slice(width, None))):
            out[:, at] = (
                dot(own[...], weight[0], NN)
                + dot(low[...], weight[3], NN)
                + dot(high[...], weight[1], NN)
            )


def input_last(
    far, value_a, state_a, value_b, state_b, own_sum, other_sum, own_ref, other_ref
):
    width = value_a.shape[2]
    for weight, at in ((value_b, slice(0, width)), (state_b, slice(width, None))):
        other_ref[:, at] = (other_sum[:, at] + dot(far[...], weight[2], NN)).astype(BF16)
    for weight, at in ((value_a, slice(0, width)), (state_a, slice(width, None))):
        own_ref[:, at] = own_sum[:, at] + dot(far[...], weight[2], NN)


def grad_first(own, low, high, out_a, out_b, own_ref, other_ref):
    for weight, out in ((out_b, other_ref), (out_a, own_ref)):
        out[...] = (
            dot(own[...], weight[0], NT)
            + dot(low[...], weight[3], NT)
            + dot(high[...], weight[1], NT)
        )


def grad_last(far, out_a, out_b, own_sum, other_sum, own_ref, other_ref):
    other_ref[...] = (other_sum[...] + dot(far[...], out_b[2], NT)).astype(BF16)
    own_ref[...] = own_sum[...] + dot(far[...], out_a[2], NT)


def masked(pair, odd):
    lane = iota(pair.shape, 1)
    keep = lane >= 64 if odd else lane < 64
    return jnp.where(keep, pair, jnp.zeros_like(pair))


def mix_kernel(
    input_sum,
    input_other,
    to_end,
    decay_ref,
    skip_ref,
    mix_ref,
    end_ref,
    local_ref,
    weight_ref,
):
    width = local_ref.shape[1]
    mix = (input_sum[...] + input_other[...].astype(F32)).astype(BF16)
    mix_ref[...] = mix
    writer = mix[:, width : width + STATE]
    reader = mix[:, width + STATE :]
    scaled = (mix[:, :width].astype(F32) * to_end[...]).astype(BF16)
    end_ref[...] = dot(writer, scaled, TN).astype(BF16)
    scores = dot(reader, writer, NT)
    for two in range(HEADS // 2):
        at = slice(two * 128, two * 128 + 128)
        value_pair = mix[:, at]
        local = value_pair.astype(F32) * skip_ref[:, at]
        for odd in range(2):
            h = 2 * two + odd
            weight = (scores * decay_ref[h].astype(F32)).astype(BF16)
            weight_ref[h] = weight
            local = local + dot(weight, masked(value_pair, odd), NN)
        local_ref[:, at] = local


def state_kernel(mix_ref, grad_sum, grad_other, entering, end_ref, totals, grad_ref, pay_ref):
    width = grad_sum.shape[1]
    grad = (grad_sum[...] + grad_other[...].astype(F32)).astype(BF16)
    grad_ref[...] = grad
    scaled = (grad.astype(F32) * entering[...]).astype(BF16)
    reader = mix_ref[:, width + STATE :]
    pay_ref[:STATE, :width] = end_ref[...]
    pay_ref[STATE:, :width] = dot(reader, scaled, TN).astype(BF16)
    total = totals[0:1, :].astype(F32)
    pay_ref[:, width:] = jnp.broadcast_to(total, (2 * STATE, 128)).astype(BF16)


def owner_kernel(pieces_ref, out_ref, decay_ref):
    count, width = out_ref.shape[0], out_ref.shape[2]
    lanes = (128, width)
    head = iota(lanes, 1) // 64
    place = iota(lanes, 0)
    keep = (place % HEADS == head) & (place < 3 * HEADS)
    totals = pieces_ref[:, 0, width:]
    decay_ref[...] = jnp.exp(dot(totals, ones_where(keep), NN))
    back = lax.axis_index("x") >= 2
    state = jnp.zeros(out_ref.shape[1:], F32)
    for k in range(count):
        at = jnp.where(back, count - 1 - k, k)
        out_ref[at] = state.astype(BF16)
        state = state * decay_ref[pl.ds(at, 1), :] + pieces_ref[at, :, :width].astype(F32)


def output_kernel(mix_ref, states_ref, entering, local_ref, out_ref):
    width = local_ref.shape[1]
    reader = mix_ref[:, width + STATE :]
    mixed = local_ref[...] + dot(reader, states_ref[:STATE, :], NN) * entering[...]
    out_ref[...] = mixed.astype(BF16)


def gradient_kernel(
    mix_ref, grad_ref, states_ref, entering, to_end, skip_ref, weight_ref, decay_ref, out_ref
):
    rows, width = grad_ref.shape
    writer = mix_ref[:, width : width + STATE]
    reader = mix_ref[:, width + STATE :]
    incoming = states_ref[:STATE, :]
    outgoing = states_ref[STATE:, :]
    score_grad = jnp.zeros((rows, rows), F32)
    for two in range(HEADS // 2):
        at = slice(two * 128, two * 128 + 128)
        value_pair = mix_ref[:, at]
        grad_pair = grad_ref[:, at]
        back = grad_pair.astype(F32) * skip_ref[:, at]
        back = back + dot(writer, outgoing[:, at], NN) * to_end[:, at]
        for odd in range(2):
            h = 2 * two + odd
            grad_one = masked(grad_pair, odd)
            back = back + dot(weight_ref[h], grad_one, TN)
            score_grad = score_grad + dot(grad_one, value_pair, NT) * decay_ref[h].astype(F32)
        out_ref[:, at] = back.astype(BF16)
    score_grad = score_grad.astype(BF16)
    value_scaled = (mix_ref[:, :width].astype(F32) * to_end[...]).astype(BF16)
    write = dot(score_grad, reader, TN) + dot(value_scaled, outgoing, NT)
    out_ref[:, width : width + STATE] = write.astype(BF16)
    grad_scaled = (grad_ref[...].astype(F32) * entering[...]).astype(BF16)
    read = dot(score_grad, writer, NN) + dot(grad_scaled, incoming, NT)
    out_ref[:, width + STATE :] = read.astype(BF16)


def output_blocks(blocks, fin, other, weight_a, weight_b, *outs):
    for out, k in zip(outs, blocks):
        total = dot(fin[...], weight_a[k], NN) + dot(other[...], weight_b[k], NN)
        out[...] = total.astype(out.dtype)


def input_blocks(blocks, fin, other, value_a, state_a, value_b, state_b, *outs):
    width = value_a.shape[2]
    for out, k in zip(outs, blocks):
        total = (
            dot(fin[:, :width], value_a[k], NT)
            + dot(fin[:, width:], state_a[k], NT)
            + dot(other[:, :width], value_b[k], NT)
            + dot(other[:, width:], state_b[k], NT)
        )
        out[...] = total.astype(out.dtype)


def add_kernel(groups, *refs):
    outs = refs[-groups:]
    count = (len(refs) - groups) // groups
    for g, out in enumerate(outs):
        total = refs[g * count][...].astype(F32)
        for ref in refs[g * count + 1 : (g + 1) * count]:
            total = total + ref[...].astype(F32)
        out[...] = total.astype(out.dtype)


def per_device(
    layer_input, value_weight, state_weight, output_weight, log_decay, skip_gain, output_grad
):
    rows, shard = layer_input.shape
    width, pair = value_weight.shape[1], state_weight.shape[1]
    wide = spec((rows, width))
    both = spec((rows, width + pair))
    block = spec((rows, shard))
    block_low = spec((rows, shard), BF16)

    input_low = shift(layer_input, "y", 1)
    input_high = shift(layer_input, "y", -1)
    grad_high = shift(output_grad, "y", -1)
    input_far = shift(input_low, "y", 1)
    grad_low = shift(output_grad, "y", 1)
    grad_far = shift(grad_high, "y", -1)

    sent = weights_of(True, value_weight, state_weight, output_weight, shard)
    value_b, state_b, out_b = [shift(w, "c", 1) for w in sent]
    value_a, state_a, out_a = weights_of(False, value_weight, state_weight, output_weight, shard)

    square = spec((HEADS, rows, rows), BF16)
    decays, entering, to_end, totals, skip = call(
        prepare_kernel,
        [square, wide, wide, spec((8, 128), BF16), spec((1, width))],
        log_decay,
        skip_gain.reshape(1, HEADS),
    )

    input_weights = (value_a, state_a, value_b, state_b)
    sums = call(
        input_first, [both, both], layer_input, input_low, input_high, *input_weights, flops=2**30
    )
    input_sum, input_send = call(
        input_last, [both, spec(both.shape, BF16)], input_far, *input_weights, *sums, flops=2**29
    )
    input_other = shift(input_send, "c", 1)
    mix, end, local, weights = call(
        mix_kernel,
        [spec((rows, width + pair), BF16), spec((STATE, width), BF16), wide, square],
        input_sum,
        input_other,
        to_end,
        decays,
        skip,
        flops=2**28,
    )
    sums = call(
        grad_first, [wide, wide], output_grad, grad_low, grad_high, out_a, out_b, flops=2**30
    )
    grad_sum, grad_send = call(
        grad_last, [wide, spec(wide.shape, BF16)], grad_far, out_a, out_b, *sums, flops=2**29
    )
    grad_other = shift(grad_send, "c", 1)
    grad, pay = call(
        state_kernel,
        [spec((rows, width), BF16), spec((2 * STATE, width + 128), BF16)],
        mix,
        grad_sum,
        grad_other,
        entering,
        end,
        totals,
    )
    pay, local = lax.optimization_barrier((pay, local))
    arrived = lax.all_to_all(pay.reshape(32, 8, width + 128), SEQ, 0, 0, tiled=True)
    owned = call(
        owner_kernel, [spec((32, 8, width), BF16)], arrived, scratch=[pltpu.VMEM((32, width), F32)]
    )[0]
    states = lax.all_to_all(owned, SEQ, 0, 0, tiled=True).reshape(2 * STATE, width)

    mixed = call(
        output_kernel, [spec((rows, width), BF16)], mix, states, entering, local, flops=2**25
    )[0]
    mixed_other = shift(mixed, "c", 1)
    grads = call(
        gradient_kernel,
        [spec((rows, width + pair), BF16)],
        mix,
        grad,
        states,
        entering,
        to_end,
        skip,
        weights,
        decays,
        flops=2**28,
    )[0]
    grads_other = shift(grads, "c", 1)

    def outputs(blocks, kinds):
        return call(
            functools.partial(output_blocks, blocks),
            kinds,
            mixed,
            mixed_other,
            out_a,
            out_b,
            flops=2**28 * len(blocks),
        )

    def inputs(blocks, kinds):
        return call(
            functools.partial(input_blocks, blocks),
            kinds,
            grads,
            grads_other,
            *input_weights,
            flops=2**28 * len(blocks),
        )

    add = functools.partial(add_kernel, 1)
    (out_2,) = outputs((2,), [block_low])
    out_from = shift(out_2, "y", 1)
    (in_2,) = inputs((2,), [block_low])
    in_from = shift(in_2, "y", -1)
    (out_3,) = outputs((3,), [block_low])
    out_high = shift(out_3, "y", -1)
    (in_1,) = inputs((1,), [block_low])
    in_low = shift(in_1, "y", 1)
    out_1, out_0 = outputs((1, 0), [block] * 2)
    in_3, in_0 = inputs((3, 0), [block] * 2)
    out_1 = call(add, [block_low], out_1, out_from)[0]
    out_low = shift(out_1, "y", 1)
    in_3 = call(add, [block_low], in_3, in_from)[0]
    in_high = shift(in_3, "y", -1)
    layer_output = call(add, [block_low], out_0, out_high, out_low)[0]
    input_grad = call(add, [block_low], in_0, in_low, in_high)[0]
    return (layer_output, input_grad)


def solution(mesh):
    split = Mesh(mesh.devices.reshape(4, 8, 4, 2), ("x", "z", "y", "c"))
    head = ("y", "c")
    in_specs = (
        P(SEQ, head),
        P(None, head),
        P(None, head),
        P(head, None),
        P(head, SEQ),
        P(head),
        P(SEQ, head),
    )
    return jax.shard_map(
        per_device,
        mesh=split,
        in_specs=in_specs,
        out_specs=(P(SEQ, head), P(SEQ, head)),
        check_vma=False,
    )
```

profile of v0, /device:TPU:2, one launch (start us, length us, event | category | flops | bytes accessed | tf_op | source)
XLA Modules:
  0.0 101.5 jit_solution(11207149514913727519)
XLA Ops:
  0.6 2.6 %shard_map.87 = (bf16[4,512,512]{2,1,0:T(8,128)(2,1)S(1)}, bf16[4,512,256]{2,1,0:T(8,128)(2,1)S(1)}, bf16[4,512,512]{2,1,0:T(8,128)(2,1)S(1)}) custom-call(bf16[4096,512]{1,0:T(8,128)(2,1)} %value_ref.3, bf16[4096,256]{1,0:T(8,128)(2,1)} %state_ref.3, bf16[512,4096]{1,0:T(8,128)(2,1)} %out_ref.3), custom_call_target="tpu_custom_call" | custom-call | bytes 10485760 | tf_op jit(solution)/shard_map/pallas_call | solution.py:140
  4.0 1.6 %collective-permute-start = (bf16[256,512]{1,0:T(8,128)(2,1)S(1)}, bf16[256,512]{1,0:T(8,128)(2,1)S(1)}, u32[]{:S(2)}, u32[]{:S(2)}) collective-permute-start(bf16[256,512]{1,0:T(8,128)(2,1)S(1)} %copy-done), channel_id=1, source_target_pairs={{0,2},{2,4},{4,6},{6,0},{1,3},{3,5},{5,7},{7,1},{8,10},{10,12},{12... | collective-permute-start | bytes 786440 | tf_op jit(solution)/shard_map/ppermute | solution.py:47
  5.6 1.7 %collective-permute-start.4 = (bf16[256,512]{1,0:T(8,128)(2,1)S(1)}, bf16[256,512]{1,0:T(8,128)(2,1)S(1)}, u32[]{:S(2)}, u32[]{:S(2)}) collective-permute-start(bf16[256,512]{1,0:T(8,128)(2,1)S(1)} %copy-done), channel_id=1, source_target_pairs={{0,6},{2,0},{4,2},{6,4},{1,7},{3,1},{5,3},{7,5},{8,14},{10,8},{12,... | collective-permute-start | bytes 786440 | tf_op jit(solution)/shard_map/ppermute | solution.py:47
  7.2 6.7 %collective-permute-done.low = bf16[256,512]{1,0:T(8,128)(2,1)S(1)} collective-permute-done((bf16[256,512]{1,0:T(8,128)(2,1)S(1)}, bf16[256,512]{1,0:T(8,128)(2,1)S(1)}, u32[]{:S(2)}, u32[]{:S(2)}) %collective-permute-start) | collective-permute-done | bytes 262176 | tf_op jit(solution)/shard_map/ppermute | solution.py:47
  13.9 1.7 %collective-permute-start.6 = (bf16[256,512]{1,0:T(8,128)(2,1)S(1)}, bf16[256,512]{1,0:T(8,128)(2,1)S(1)}, u32[]{:S(2)}, u32[]{:S(2)}) collective-permute-start(bf16[256,512]{1,0:T(8,128)(2,1)S(1)} %copy-done.1), channel_id=1, source_target_pairs={{0,6},{2,0},{4,2},{6,4},{1,7},{3,1},{5,3},{7,5},{8,14},{10,8},{12,... | collective-permute-start | bytes 786440 | tf_op jit(solution)/shard_map/ppermute | solution.py:47
  15.9 5.8 %collective-permute-done.6.high = bf16[256,512]{1,0:T(8,128)(2,1)S(1)} collective-permute-done((bf16[256,512]{1,0:T(8,128)(2,1)S(1)}, bf16[256,512]{1,0:T(8,128)(2,1)S(1)}, u32[]{:S(2)}, u32[]{:S(2)}) %collective-permute-start.6) | collective-permute-done | bytes 262176 | tf_op jit(solution)/shard_map/ppermute | solution.py:47
  22.0 3.0 %collective-permute-start.7 = (bf16[256,512]{1,0:T(8,128)(2,1)S(1)}, bf16[256,512]{1,0:T(8,128)(2,1)S(1)}, u32[]{:S(2)}, u32[]{:S(2)}) collective-permute-start(bf16[256,512]{1,0:T(8,128)(2,1)S(1)} %collective-permute-done.6.high), channel_id=1, source_target_pairs={{0,6},{2,0},{4,2},{6,4},{1,7},{3,1},{5,3},{7,5},{8,14},{10,8},{12,... | collective-permute-start | bytes 786440 | tf_op jit(solution)/shard_map/ppermute | solution.py:47
  25.0 2.6 %shard_map.86 = (bf16[4,512,512]{2,1,0:T(8,128)(2,1)S(1)}, bf16[4,512,256]{2,1,0:T(8,128)(2,1)S(1)}, bf16[4,512,512]{2,1,0:T(8,128)(2,1)S(1)}) custom-call(bf16[4096,512]{1,0:T(8,128)(2,1)} %value_ref.3, bf16[4096,256]{1,0:T(8,128)(2,1)} %state_ref.3, bf16[512,4096]{1,0:T(8,128)(2,1)} %out_ref.3), custom_call_target="tpu_custom_call" | custom-call | bytes 10485760 | tf_op jit(solution)/shard_map/pallas_call | solution.py:140
  27.6 1.4 %shard_map.88 = (f32[256,768]{1,0:T(8,128)S(1)}, f32[256,768]{1,0:T(8,128)S(1)}) custom-call(bf16[256,512]{1,0:T(8,128)(2,1)S(1)} %copy-done, bf16[256,512]{1,0:T(8,128)(2,1)S(1)} %collective-permute-done.low, bf16[256,512]{1,0:T(8,128)(2,1)S(1)} %collective-permute-done.4.high, bf16[4,512,512]{2,1,0:T(8,128)(2,1)S(1)} %get-tuple-element.33.value_a, ...), custom_call_target="tpu_custom_call" | custom-call | flops 1073741824 | bytes 8650752 | tf_op jit(solution)/shard_map/pallas_call | solution.py:34
  29.0 0.6 shard_map.89
  30.0 1.0 shard_map.92
  31.8 1.4 %shard_map.90 = (bf16[8,256,256]{2,1,0:T(8,128)(2,1)S(1)}, f32[256,512]{1,0:T(8,128)S(1)}, f32[256,512]{1,0:T(8,128)S(1)}, bf16[8,128]{1,0:T(8,128)(2,1)S(1)}, f32[1,512]{1,0:T(1,128)S(1)}) custom-call(f32[8,256]{1,0:T(8,128)S(1)} %copy-done.2, f32[1,8]{1,0:T(1,128)S(1)} %bitcast.6), custom_call_target="tpu_custom_call" | custom-call | flops 16777216 | bytes 2109472 | tf_op jit(solution)/shard_map/pallas_call | solution.py:34
  33.2 0.6 shard_map.91
  34.1 23.8 %all_to_all.10.pieces_ref = bf16[32,8,640]{2,1,0:T(8,128)(2,1)S(1)} all-to-all(bf16[32,8,640]{2,1,0:T(8,128)(2,1)S(1)} %bitcast.5), channel_id=1, replica_groups=mesh['x'=4,'z'=8,'y'=4,'c'=2] {'x','z'}, dimensions={0} | all-to-all | bytes 655360 | tf_op jit(solution)/shard_map/all_to_all | solution.py:383
  58.1 17.1 %all_to_all.11 = bf16[32,8,512]{2,1,0:T(8,128)(2,1)S(1)} all-to-all(bf16[32,8,512]{2,1,0:T(8,128)(2,1)S(1)} %shard_map.95), channel_id=1, replica_groups=mesh['x'=4,'z'=8,'y'=4,'c'=2] {'x','z'}, dimensions={0} | all-to-all | bytes 524288 | tf_op jit(solution)/shard_map/all_to_all | solution.py:387
  75.2 1.1 %shard_map.102.fin = bf16[256,768]{1,0:T(8,128)(2,1)S(1)} custom-call(bf16[256,768]{1,0:T(8,128)(2,1)S(1)} %get-tuple-element.44.mix_ref, bf16[256,512]{1,0:T(8,128)(2,1)S(1)} %get-tuple-element.60.grad_ref, bf16[256,512]{1,0:T(8,128)(2,1)S(1)} %bitcast.3, f32[256,512]{1,0:T(8,128)S(1)} %get-tuple-element.51.entering, ...), custom_call_target="tpu_custom_call" | custom-call | flops 268435456 | bytes 4458496 | tf_op jit(solution)/shard_map/pallas_call | solution.py:34
  76.7 0.6 collective-permute-start.11
  77.2 1.3 %collective-permute-done.11.other = bf16[256,512]{1,0:T(8,128)(2,1)S(1)} collective-permute-done((bf16[256,512]{1,0:T(8,128)(2,1)S(1)}, bf16[256,512]{1,0:T(8,128)(2,1)S(1)}, u32[]{:S(2)}, u32[]{:S(2)}) %collective-permute-start.11) | collective-permute-done | bytes 262176 | tf_op jit(solution)/shard_map/ppermute | solution.py:47
  79.1 0.6 shard_map.105
  79.7 3.3 %collective-permute-start.17 = (bf16[256,512]{1,0:T(8,128)(2,1)S(1)}, bf16[256,512]{1,0:T(8,128)(2,1)S(1)}, u32[]{:S(2)}, u32[]{:S(2)}) collective-permute-start(bf16[256,512]{1,0:T(8,128)(2,1)S(1)} %shard_map.105), channel_id=1, source_target_pairs={{0,6},{2,0},{4,2},{6,4},{1,7},{3,1},{5,3},{7,5},{8,14},{10,8},{12,... | collective-permute-start | bytes 786440 | tf_op jit(solution)/shard_map/ppermute | solution.py:47
  83.4 0.7 collective-permute-start.12
  84.1 0.7 shard_map.97
  84.8 0.6 shard_map.104
  85.4 1.5 %collective-permute-start.16 = (bf16[256,512]{1,0:T(8,128)(2,1)S(1)}, bf16[256,512]{1,0:T(8,128)(2,1)S(1)}, u32[]{:S(2)}, u32[]{:S(2)}) collective-permute-start(bf16[256,512]{1,0:T(8,128)(2,1)S(1)} %shard_map.104), channel_id=1, source_target_pairs={{0,2},{2,4},{4,6},{6,0},{1,3},{3,5},{5,7},{7,1},{8,10},{10,12},{12... | collective-permute-start | bytes 786440 | tf_op jit(solution)/shard_map/ppermute | solution.py:47
  86.9 1.0 shard_map.103
  87.9 0.8 collective-permute-done.13.refs_1_
  88.9 0.8 collective-permute-done.17.refs_1_
  89.7 3.8 %collective-permute-start.18 = (bf16[256,512]{1,0:T(8,128)(2,1)S(1)}, bf16[256,512]{1,0:T(8,128)(2,1)S(1)}, u32[]{:S(2)}, u32[]{:S(2)}) collective-permute-start(bf16[256,512]{1,0:T(8,128)(2,1)S(1)} %shard_map.106), channel_id=1, source_target_pairs={{0,6},{2,0},{4,2},{6,4},{1,7},{3,1},{5,3},{7,5},{8,14},{10,8},{12,... | collective-permute-start | bytes 786440 | tf_op jit(solution)/shard_map/ppermute | solution.py:47
  93.5 1.8 %collective-permute-done.12.refs_1_ = bf16[256,512]{1,0:T(8,128)(2,1)S(1)} collective-permute-done((bf16[256,512]{1,0:T(8,128)(2,1)S(1)}, bf16[256,512]{1,0:T(8,128)(2,1)S(1)}, u32[]{:S(2)}, u32[]{:S(2)}) %collective-permute-start.12) | collective-permute-done | bytes 262176 | tf_op jit(solution)/shard_map/ppermute | solution.py:47
  95.3 4.7 %collective-permute-done.14.refs_2_ = bf16[256,512]{1,0:T(8,128)(2,1)S(1)} collective-permute-done((bf16[256,512]{1,0:T(8,128)(2,1)S(1)}, bf16[256,512]{1,0:T(8,128)(2,1)S(1)}, u32[]{:S(2)}, u32[]{:S(2)}) %collective-permute-start.14) | collective-permute-done | bytes 262176 | tf_op jit(solution)/shard_map/ppermute | solution.py:47
  100.0 0.8 shard_map.101
  100.8 0.8 shard_map.107
  (38 shorter events, 4.3 us)
Async XLA Ops:
  0.6 3.4 %copy-start = (bf16[256,512]{1,0:T(8,128)(2,1)S(1)}, bf16[256,512]{1,0:T(8,128)(2,1)}, u32[]{:S(2)}) copy-start(bf16[256,512]{1,0:T(8,128)(2,1)} %own.2) | copy-start | bytes 786436
  0.6 13.3 %copy-start.1 = (bf16[256,512]{1,0:T(8,128)(2,1)S(1)}, bf16[256,512]{1,0:T(8,128)(2,1)}, u32[]{:S(2)}) copy-start(bf16[256,512]{1,0:T(8,128)(2,1)} %own.3) | copy-start | bytes 786436
  3.3 24.3 %collective-permute-start.2 = (bf16[4,512,512]{2,1,0:T(8,128)(2,1)S(1)}, bf16[4,512,512]{2,1,0:T(8,128)(2,1)S(1)}, u32[]{:S(2)}, u32[]{:S(2)}) collective-permute-start(bf16[4,512,512]{2,1,0:T(8,128)(2,1)S(1)} %get-tuple-element.35), channel_id=1, source_target_pairs={{0,1},{1,0},{2,3},{3,2},{4,5},{5,4},{6,7},{7,6},{8,9},{9,8},{10,11... | collective-permute-start | bytes 6291464 | tf_op jit(solution)/shard_map/ppermute | solution.py:47
  3.4 26.6 %collective-permute-start.8 = (bf16[4,512,512]{2,1,0:T(8,128)(2,1)S(1)}, bf16[4,512,512]{2,1,0:T(8,128)(2,1)S(1)}, u32[]{:S(2)}, u32[]{:S(2)}) collective-permute-start(bf16[4,512,512]{2,1,0:T(8,128)(2,1)S(1)} %get-tuple-element.46), channel_id=1, source_target_pairs={{0,1},{1,0},{2,3},{3,2},{4,5},{5,4},{6,7},{7,6},{8,9},{9,8},{10,11... | collective-permute-start | bytes 6291464 | tf_op jit(solution)/shard_map/ppermute | solution.py:47
  3.9 18.1 %collective-permute-start.3 = (bf16[4,512,256]{2,1,0:T(8,128)(2,1)S(1)}, bf16[4,512,256]{2,1,0:T(8,128)(2,1)S(1)}, u32[]{:S(2)}, u32[]{:S(2)}) collective-permute-start(bf16[4,512,256]{2,1,0:T(8,128)(2,1)S(1)} %get-tuple-element.36), channel_id=1, source_target_pairs={{0,1},{1,0},{2,3},{3,2},{4,5},{5,4},{6,7},{7,6},{8,9},{9,8},{10,11... | collective-permute-start | bytes 3145736 | tf_op jit(solution)/shard_map/ppermute | solution.py:47
  4.0 9.9 %collective-permute-start = (bf16[256,512]{1,0:T(8,128)(2,1)S(1)}, bf16[256,512]{1,0:T(8,128)(2,1)S(1)}, u32[]{:S(2)}, u32[]{:S(2)}) collective-permute-start(bf16[256,512]{1,0:T(8,128)(2,1)S(1)} %copy-done), channel_id=1, source_target_pairs={{0,2},{2,4},{4,6},{6,0},{1,3},{3,5},{5,7},{7,1},{8,10},{10,12},{12... | collective-permute-start | bytes 786440 | tf_op jit(solution)/shard_map/ppermute | solution.py:47
  5.6 10.1 %collective-permute-start.4 = (bf16[256,512]{1,0:T(8,128)(2,1)S(1)}, bf16[256,512]{1,0:T(8,128)(2,1)S(1)}, u32[]{:S(2)}, u32[]{:S(2)}) collective-permute-start(bf16[256,512]{1,0:T(8,128)(2,1)S(1)} %copy-done), channel_id=1, source_target_pairs={{0,6},{2,0},{4,2},{6,4},{1,7},{3,1},{5,3},{7,5},{8,14},{10,8},{12,... | collective-permute-start | bytes 786440 | tf_op jit(solution)/shard_map/ppermute | solution.py:47
  13.9 7.8 %collective-permute-start.6 = (bf16[256,512]{1,0:T(8,128)(2,1)S(1)}, bf16[256,512]{1,0:T(8,128)(2,1)S(1)}, u32[]{:S(2)}, u32[]{:S(2)}) collective-permute-start(bf16[256,512]{1,0:T(8,128)(2,1)S(1)} %copy-done.1), channel_id=1, source_target_pairs={{0,6},{2,0},{4,2},{6,4},{1,7},{3,1},{5,3},{7,5},{8,14},{10,8},{12,... | collective-permute-start | bytes 786440 | tf_op jit(solution)/shard_map/ppermute | solution.py:47
  15.6 13.3 %collective-permute-start.1 = (bf16[256,512]{1,0:T(8,128)(2,1)S(1)}, bf16[256,512]{1,0:T(8,128)(2,1)S(1)}, u32[]{:S(2)}, u32[]{:S(2)}) collective-permute-start(bf16[256,512]{1,0:T(8,128)(2,1)S(1)} %collective-permute-done.low), channel_id=1, source_target_pairs={{0,2},{2,4},{4,6},{6,0},{1,3},{3,5},{5,7},{7,1},{8,10},{10,12},{12... | collective-permute-start | bytes 786440 | tf_op jit(solution)/shard_map/ppermute | solution.py:47
  21.7 8.2 %collective-permute-start.9 = (bf16[256,512]{1,0:T(8,128)(2,1)S(1)}, bf16[256,512]{1,0:T(8,128)(2,1)S(1)}, u32[]{:S(2)}, u32[]{:S(2)}) collective-permute-start(bf16[256,512]{1,0:T(8,128)(2,1)S(1)} %copy-done.1), channel_id=1, source_target_pairs={{0,2},{2,4},{4,6},{6,0},{1,3},{3,5},{5,7},{7,1},{8,10},{10,12},{12... | collective-permute-start | bytes 786440 | tf_op jit(solution)/shard_map/ppermute | solution.py:47
  22.0 9.0 %collective-permute-start.7 = (bf16[256,512]{1,0:T(8,128)(2,1)S(1)}, bf16[256,512]{1,0:T(8,128)(2,1)S(1)}, u32[]{:S(2)}, u32[]{:S(2)}) collective-permute-start(bf16[256,512]{1,0:T(8,128)(2,1)S(1)} %collective-permute-done.6.high), channel_id=1, source_target_pairs={{0,6},{2,0},{4,2},{6,4},{1,7},{3,1},{5,3},{7,5},{8,14},{10,8},{12,... | collective-permute-start | bytes 786440 | tf_op jit(solution)/shard_map/ppermute | solution.py:47
  29.5 3.6 %collective-permute-start.5 = (bf16[256,768]{1,0:T(8,128)(2,1)S(1)}, bf16[256,768]{1,0:T(8,128)(2,1)S(1)}, u32[]{:S(2)}, u32[]{:S(2)}) collective-permute-start(bf16[256,768]{1,0:T(8,128)(2,1)S(1)} %get-tuple-element.40), channel_id=1, source_target_pairs={{0,1},{1,0},{2,3},{3,2},{4,5},{5,4},{6,7},{7,6},{8,9},{9,8},{10,11... | collective-permute-start | bytes 1179656 | tf_op jit(solution)/shard_map/ppermute | solution.py:47
  31.0 0.8 copy-start.2
  31.0 0.8 copy-start.3
  31.5 2.3 %collective-permute-start.10 = (bf16[256,512]{1,0:T(8,128)(2,1)S(1)}, bf16[256,512]{1,0:T(8,128)(2,1)S(1)}, u32[]{:S(2)}, u32[]{:S(2)}) collective-permute-start(bf16[256,512]{1,0:T(8,128)(2,1)S(1)} %get-tuple-element.50), channel_id=1, source_target_pairs={{0,1},{1,0},{2,3},{3,2},{4,5},{5,4},{6,7},{7,6},{8,9},{9,8},{10,11... | collective-permute-start | bytes 786440 | tf_op jit(solution)/shard_map/ppermute | solution.py:47
  76.3 2.7 %collective-permute-start.15 = (bf16[256,768]{1,0:T(8,128)(2,1)S(1)}, bf16[256,768]{1,0:T(8,128)(2,1)S(1)}, u32[]{:S(2)}, u32[]{:S(2)}) collective-permute-start(bf16[256,768]{1,0:T(8,128)(2,1)S(1)} %shard_map.102.fin), channel_id=1, source_target_pairs={{0,1},{1,0},{2,3},{3,2},{4,5},{5,4},{6,7},{7,6},{8,9},{9,8},{10,11... | collective-permute-start | bytes 1179656 | tf_op jit(solution)/shard_map/ppermute | solution.py:47
  76.7 1.9 %collective-permute-start.11 = (bf16[256,512]{1,0:T(8,128)(2,1)S(1)}, bf16[256,512]{1,0:T(8,128)(2,1)S(1)}, u32[]{:S(2)}, u32[]{:S(2)}) collective-permute-start(bf16[256,512]{1,0:T(8,128)(2,1)S(1)} %shard_map.96.fin), channel_id=1, source_target_pairs={{0,1},{1,0},{2,3},{3,2},{4,5},{5,4},{6,7},{7,6},{8,9},{9,8},{10,11... | collective-permute-start | bytes 786440 | tf_op jit(solution)/shard_map/ppermute | solution.py:47
  79.0 9.8 %collective-permute-start.13 = (bf16[256,512]{1,0:T(8,128)(2,1)S(1)}, bf16[256,512]{1,0:T(8,128)(2,1)S(1)}, u32[]{:S(2)}, u32[]{:S(2)}) collective-permute-start(bf16[256,512]{1,0:T(8,128)(2,1)S(1)} %shard_map.99), channel_id=1, source_target_pairs={{0,2},{2,4},{4,6},{6,0},{1,3},{3,5},{5,7},{7,1},{8,10},{10,12},{12... | collective-permute-start | bytes 786440 | tf_op jit(solution)/shard_map/ppermute | solution.py:47
  79.7 10.0 %collective-permute-start.17 = (bf16[256,512]{1,0:T(8,128)(2,1)S(1)}, bf16[256,512]{1,0:T(8,128)(2,1)S(1)}, u32[]{:S(2)}, u32[]{:S(2)}) collective-permute-start(bf16[256,512]{1,0:T(8,128)(2,1)S(1)} %shard_map.105), channel_id=1, source_target_pairs={{0,6},{2,0},{4,2},{6,4},{1,7},{3,1},{5,3},{7,5},{8,14},{10,8},{12,... | collective-permute-start | bytes 786440 | tf_op jit(solution)/shard_map/ppermute | solution.py:47
  83.4 11.9 %collective-permute-start.12 = (bf16[256,512]{1,0:T(8,128)(2,1)S(1)}, bf16[256,512]{1,0:T(8,128)(2,1)S(1)}, u32[]{:S(2)}, u32[]{:S(2)}) collective-permute-start(bf16[256,512]{1,0:T(8,128)(2,1)S(1)} %shard_map.98), channel_id=1, source_target_pairs={{0,6},{2,0},{4,2},{6,4},{1,7},{3,1},{5,3},{7,5},{8,14},{10,8},{12,... | collective-permute-start | bytes 786440 | tf_op jit(solution)/shard_map/ppermute | solution.py:47
  85.4 15.3 %collective-permute-start.16 = (bf16[256,512]{1,0:T(8,128)(2,1)S(1)}, bf16[256,512]{1,0:T(8,128)(2,1)S(1)}, u32[]{:S(2)}, u32[]{:S(2)}) collective-permute-start(bf16[256,512]{1,0:T(8,128)(2,1)S(1)} %shard_map.104), channel_id=1, source_target_pairs={{0,2},{2,4},{4,6},{6,0},{1,3},{3,5},{5,7},{7,1},{8,10},{10,12},{12... | collective-permute-start | bytes 786440 | tf_op jit(solution)/shard_map/ppermute | solution.py:47
  88.8 11.2 %collective-permute-start.14 = (bf16[256,512]{1,0:T(8,128)(2,1)S(1)}, bf16[256,512]{1,0:T(8,128)(2,1)S(1)}, u32[]{:S(2)}, u32[]{:S(2)}) collective-permute-start(bf16[256,512]{1,0:T(8,128)(2,1)S(1)} %shard_map.100), channel_id=1, source_target_pairs={{0,2},{2,4},{4,6},{6,0},{1,3},{3,5},{5,7},{7,1},{8,10},{10,12},{12... | collective-permute-start | bytes 786440 | tf_op jit(solution)/shard_map/ppermute | solution.py:47
  89.7 11.0 %collective-permute-start.18 = (bf16[256,512]{1,0:T(8,128)(2,1)S(1)}, bf16[256,512]{1,0:T(8,128)(2,1)S(1)}, u32[]{:S(2)}, u32[]{:S(2)}) collective-permute-start(bf16[256,512]{1,0:T(8,128)(2,1)S(1)} %shard_map.106), channel_id=1, source_target_pairs={{0,6},{2,0},{4,2},{6,4},{1,7},{3,1},{5,3},{7,5},{8,14},{10,8},{12,... | collective-permute-start | bytes 786440 | tf_op jit(solution)/shard_map/ppermute | solution.py:47
where the time goes:
time: 102 us
  blocking collectives  40.9 us (40%)
  waiting for transfers between devices  22.2 us (22%)
  starting transfers between devices  19.6 us (19%)
  Pallas kernels  17.9 us (18%)
    all_to_all x1, blocking collectives, per_device(): lax.all_to_all(pay.reshape(32, 8, width + 128), SEQ, 0, 0, tiled=True)  23.8 us
    ppermute x19, waiting for transfers between devices, shift(): lax.ppermute(array, axis, [(i, (i + step) % size) for i in range(size)])  22.2 us
    ppermute x19, starting transfers between devices, shift(): lax.ppermute(array, axis, [(i, (i + step) % size) for i in range(size)])  19.6 us
    all_to_all x1, blocking collectives, per_device(): lax.all_to_all(owned, SEQ, 0, 0, tiled=True).reshape(2 * STATE, width)  17.1 us
    pallas_call x20, Pallas kernels, call(): pl.pallas_call(body, out_shape=outs, in_specs=[vmem] * len(args), out_spe...  12.7 us
    pallas_call x2, Pallas kernels, weights_of(): pl.pallas_call(functools.partial(weights_kernel, other), out_shape=[spec(...  5.22 us
  transfers between devices with their start and end apart: 19, of which 8 were waited for; matrix products, arithmetic and copies ran while one was open for 0% of the time, Pallas kernels for 13%

commit v1 on v0

--- a/solution.py
+++ b/solution.py
@@ -45,6 +45,15 @@
 def shift(array, axis, step):
     size = lax.axis_size(axis)
     return lax.ppermute(array, axis, [(i, (i + step) % size) for i in range(size)])
+
+
+def ring(array, sign):
+    pairs = []
+    for y in range(4):
+        for c in range(2):
+            step = sign * (1 - 2 * c)
+            pairs.append((2 * y + c, 2 * ((y + step) % 4) + c))
+    return lax.ppermute(array, ("y", "c"), pairs)
 
 
 def parts_of(array):
@@ -287,15 +296,22 @@
     out_ref[:, width + STATE :] = read.astype(BF16)
 
 
+def resolved(block):
+    c = lax.axis_index("c")
+    return {"A": 3 - 2 * c, "B": 1 + 2 * c}.get(block, block)
+
+
 def output_blocks(blocks, fin, other, weight_a, weight_b, *outs):
-    for out, k in zip(outs, blocks):
+    for out, block in zip(outs, blocks):
+        k = resolved(block)
         total = dot(fin[...], weight_a[k], NN) + dot(other[...], weight_b[k], NN)
         out[...] = total.astype(out.dtype)
 
 
 def input_blocks(blocks, fin, other, value_a, state_a, value_b, state_b, *outs):
     width = value_a.shape[2]
-    for out, k in zip(outs, blocks):
+    for out, block in zip(outs, blocks):
+        k = resolved(block)
         total = (
             dot(fin[:, :width], value_a[k], NT)
             + dot(fin[:, width:], state_a[k], NT)
@@ -428,21 +444,21 @@
 
     add = functools.partial(add_kernel, 1)
     (out_2,) = outputs((2,), [block_low])
-    out_from = shift(out_2, "y", 1)
+    out_from = ring(out_2, 1)
     (in_2,) = inputs((2,), [block_low])
-    in_from = shift(in_2, "y", -1)
-    (out_3,) = outputs((3,), [block_low])
-    out_high = shift(out_3, "y", -1)
-    (in_1,) = inputs((1,), [block_low])
-    in_low = shift(in_1, "y", 1)
-    out_1, out_0 = outputs((1, 0), [block] * 2)
-    in_3, in_0 = inputs((3, 0), [block] * 2)
-    out_1 = call(add, [block_low], out_1, out_from)[0]
-    out_low = shift(out_1, "y", 1)
-    in_3 = call(add, [block_low], in_3, in_from)[0]
-    in_high = shift(in_3, "y", -1)
-    layer_output = call(add, [block_low], out_0, out_high, out_low)[0]
-    input_grad = call(add, [block_low], in_0, in_low, in_high)[0]
+    in_from = ring(in_2, 1)
+    (out_a_block,) = outputs(("A",), [block_low])
+    out_near = ring(out_a_block, -1)
+    (in_a_block,) = inputs(("A",), [block_low])
+    in_near = ring(in_a_block, -1)
+    out_b_block, out_0 = outputs(("B", 0), [block] * 2)
+    in_b_block, in_0 = inputs(("B", 0), [block] * 2)
+    out_b_block = call(add, [block_low], out_b_block, out_from)[0]
+    out_last = ring(out_b_block, 1)
+    in_b_block = call(add, [block_low], in_b_block, in_from)[0]
+    in_last = ring(in_b_block, 1)
+    layer_output = call(add, [block_low], out_0, out_near, out_last)[0]
+    input_grad = call(add, [block_low], in_0, in_near, in_last)[0]
     return (layer_output, input_grad)
 
 

time: 102 us -> 102 us (level)
  starting transfers between devices: 19.6 us -> 16 us
  waiting for transfers between devices: 22.2 us -> 25.7 us
    ppermute x0 -> x6, waiting for transfers between devices: none -> 11.6 us  [ring(): return lax.ppermute(array, ('y', 'c'), pairs)]
    ppermute x19 -> x13, starting transfers between devices: 19.6 us -> 10.2 us  [shift(): lax.ppermute(array, axis, [(i, (i + step) % size) for i in range(size)])]
    ppermute x19 -> x13, waiting for transfers between devices: 22.2 us -> 14.1 us  [shift(): lax.ppermute(array, axis, [(i, (i + step) % size) for i in range(size)])]
    ppermute x0 -> x6, starting transfers between devices: none -> 5.74 us  [ring(): return lax.ppermute(array, ('y', 'c'), pairs)]
  transfers between devices with their start and end apart: 19 -> 19, of which waited for: 8 -> 7; matrix products, arithmetic and copies ran while one was open for 0% -> 0% of each run, Pallas kernels for 13% -> 13%
where the time goes in v1:
time: 102 us; the launch traced here: 101 us
  blocking collectives  40.9 us (40%)
  waiting for transfers between devices  25.7 us (25%)
  Pallas kernels  17.9 us (18%)
  starting transfers between devices  16 us (16%)
    all_to_all x1, blocking collectives, per_device(): lax.all_to_all(pay.reshape(32, 8, width + 128), SEQ, 0, 0, tiled=True)  23.8 us
    all_to_all x1, blocking collectives, per_device(): lax.all_to_all(owned, SEQ, 0, 0, tiled=True).reshape(2 * STATE, width)  17.1 us
    ppermute x13, waiting for transfers between devices, shift(): lax.ppermute(array, axis, [(i, (i + step) % size) for i in range(size)])  14.1 us
    pallas_call x20, Pallas kernels, call(): pl.pallas_call(body, out_shape=outs, in_specs=[vmem] * len(args), out_spe...  12.7 us
    ppermute x6, waiting for transfers between devices, ring(): return lax.ppermute(array, ('y', 'c'), pairs)  11.6 us
    ppermute x13, starting transfers between devices, shift(): lax.ppermute(array, axis, [(i, (i + step) % size) for i in range(size)])  10.2 us
    ppermute x6, starting transfers between devices, ring(): return lax.ppermute(array, ('y', 'c'), pairs)  5.74 us
    pallas_call x2, Pallas kernels, weights_of(): pl.pallas_call(functools.partial(weights_kernel, other), out_shape=[spec(...  5.22 us
  transfers between devices with their start and end apart: 19, of which 7 were waited for; matrix products, arithmetic and copies ran while one was open for 0% of the time, Pallas kernels for 13%

profile of v1, /device:TPU:2, one launch (start us, length us, event | category | flops | bytes accessed | tf_op | source)
XLA Modules:
  0.0 101.4 jit_solution(12028147727831175327)
XLA Ops:
  0.6 2.6 %shard_map.87 = (bf16[4,512,512]{2,1,0:T(8,128)(2,1)S(1)}, bf16[4,512,256]{2,1,0:T(8,128)(2,1)S(1)}, bf16[4,512,512]{2,1,0:T(8,128)(2,1)S(1)}) custom-call(bf16[4096,512]{1,0:T(8,128)(2,1)} %value_ref.3, bf16[4096,256]{1,0:T(8,128)(2,1)} %state_ref.3, bf16[512,4096]{1,0:T(8,128)(2,1)} %out_ref.3), custom_call_target="tpu_custom_call" | custom-call | bytes 10485760 | tf_op jit(solution)/shard_map/pallas_call | solution.py:149
  3.4 0.5 collective-permute-start.8
  4.0 1.6 %collective-permute-start = (bf16[256,512]{1,0:T(8,128)(2,1)S(1)}, bf16[256,512]{1,0:T(8,128)(2,1)S(1)}, u32[]{:S(2)}, u32[]{:S(2)}) collective-permute-start(bf16[256,512]{1,0:T(8,128)(2,1)S(1)} %copy-done), channel_id=1, source_target_pairs={{0,2},{2,4},{4,6},{6,0},{1,3},{3,5},{5,7},{7,1},{8,10},{10,12},{12... | collective-permute-start | bytes 786440 | tf_op jit(solution)/shard_map/ppermute | solution.py:47
  5.6 1.7 %collective-permute-start.4 = (bf16[256,512]{1,0:T(8,128)(2,1)S(1)}, bf16[256,512]{1,0:T(8,128)(2,1)S(1)}, u32[]{:S(2)}, u32[]{:S(2)}) collective-permute-start(bf16[256,512]{1,0:T(8,128)(2,1)S(1)} %copy-done), channel_id=1, source_target_pairs={{0,6},{2,0},{4,2},{6,4},{1,7},{3,1},{5,3},{7,5},{8,14},{10,8},{12,... | collective-permute-start | bytes 786440 | tf_op jit(solution)/shard_map/ppermute | solution.py:47
  7.2 6.7 %collective-permute-done.low = bf16[256,512]{1,0:T(8,128)(2,1)S(1)} collective-permute-done((bf16[256,512]{1,0:T(8,128)(2,1)S(1)}, bf16[256,512]{1,0:T(8,128)(2,1)S(1)}, u32[]{:S(2)}, u32[]{:S(2)}) %collective-permute-start) | collective-permute-done | bytes 262176 | tf_op jit(solution)/shard_map/ppermute | solution.py:47
  13.9 1.7 %collective-permute-start.6 = (bf16[256,512]{1,0:T(8,128)(2,1)S(1)}, bf16[256,512]{1,0:T(8,128)(2,1)S(1)}, u32[]{:S(2)}, u32[]{:S(2)}) collective-permute-start(bf16[256,512]{1,0:T(8,128)(2,1)S(1)} %copy-done.1), channel_id=1, source_target_pairs={{0,6},{2,0},{4,2},{6,4},{1,7},{3,1},{5,3},{7,5},{8,14},{10,8},{12,... | collective-permute-start | bytes 786440 | tf_op jit(solution)/shard_map/ppermute | solution.py:47
  15.9 5.8 %collective-permute-done.6.high = bf16[256,512]{1,0:T(8,128)(2,1)S(1)} collective-permute-done((bf16[256,512]{1,0:T(8,128)(2,1)S(1)}, bf16[256,512]{1,0:T(8,128)(2,1)S(1)}, u32[]{:S(2)}, u32[]{:S(2)}) %collective-permute-start.6) | collective-permute-done | bytes 262176 | tf_op jit(solution)/shard_map/ppermute | solution.py:47
  22.0 3.0 %collective-permute-start.7 = (bf16[256,512]{1,0:T(8,128)(2,1)S(1)}, bf16[256,512]{1,0:T(8,128)(2,1)S(1)}, u32[]{:S(2)}, u32[]{:S(2)}) collective-permute-start(bf16[256,512]{1,0:T(8,128)(2,1)S(1)} %collective-permute-done.6.high), channel_id=1, source_target_pairs={{0,6},{2,0},{4,2},{6,4},{1,7},{3,1},{5,3},{7,5},{8,14},{10,8},{12,... | collective-permute-start | bytes 786440 | tf_op jit(solution)/shard_map/ppermute | solution.py:47
  25.0 2.6 %shard_map.86 = (bf16[4,512,512]{2,1,0:T(8,128)(2,1)S(1)}, bf16[4,512,256]{2,1,0:T(8,128)(2,1)S(1)}, bf16[4,512,512]{2,1,0:T(8,128)(2,1)S(1)}) custom-call(bf16[4096,512]{1,0:T(8,128)(2,1)} %value_ref.3, bf16[4096,256]{1,0:T(8,128)(2,1)} %state_ref.3, bf16[512,4096]{1,0:T(8,128)(2,1)} %out_ref.3), custom_call_target="tpu_custom_call" | custom-call | bytes 10485760 | tf_op jit(solution)/shard_map/pallas_call | solution.py:149
  27.6 1.4 %shard_map.88 = (f32[256,768]{1,0:T(8,128)S(1)}, f32[256,768]{1,0:T(8,128)S(1)}) custom-call(bf16[256,512]{1,0:T(8,128)(2,1)S(1)} %copy-done, bf16[256,512]{1,0:T(8,128)(2,1)S(1)} %collective-permute-done.low, bf16[256,512]{1,0:T(8,128)(2,1)S(1)} %collective-permute-done.4.high, bf16[4,512,512]{2,1,0:T(8,128)(2,1)S(1)} %get-tuple-element.33.value_a, ...), custom_call_target="tpu_custom_call" | custom-call | flops 1073741824 | bytes 8650752 | tf_op jit(solution)/shard_map/pallas_call | solution.py:34
  29.0 0.6 shard_map.89
  30.0 1.0 shard_map.92
  31.0 0.5 shard_map.93
  31.8 1.4 %shard_map.90 = (bf16[8,256,256]{2,1,0:T(8,128)(2,1)S(1)}, f32[256,512]{1,0:T(8,128)S(1)}, f32[256,512]{1,0:T(8,128)S(1)}, bf16[8,128]{1,0:T(8,128)(2,1)S(1)}, f32[1,512]{1,0:T(1,128)S(1)}) custom-call(f32[8,256]{1,0:T(8,128)S(1)} %copy-done.2, f32[1,8]{1,0:T(1,128)S(1)} %bitcast.6), custom_call_target="tpu_custom_call" | custom-call | flops 16777216 | bytes 2109472 | tf_op jit(solution)/shard_map/pallas_call | solution.py:34
  33.2 0.6 shard_map.91
  34.1 23.8 %all_to_all.10.pieces_ref = bf16[32,8,640]{2,1,0:T(8,128)(2,1)S(1)} all-to-all(bf16[32,8,640]{2,1,0:T(8,128)(2,1)S(1)} %bitcast.5), channel_id=1, replica_groups=mesh['x'=4,'z'=8,'y'=4,'c'=2] {'x','z'}, dimensions={0} | all-to-all | bytes 655360 | tf_op jit(solution)/shard_map/all_to_all | solution.py:399
  58.1 17.1 %all_to_all.11 = bf16[32,8,512]{2,1,0:T(8,128)(2,1)S(1)} all-to-all(bf16[32,8,512]{2,1,0:T(8,128)(2,1)S(1)} %shard_map.95), channel_id=1, replica_groups=mesh['x'=4,'z'=8,'y'=4,'c'=2] {'x','z'}, dimensions={0} | all-to-all | bytes 524288 | tf_op jit(solution)/shard_map/all_to_all | solution.py:403
  75.2 1.1 %shard_map.102.fin = bf16[256,768]{1,0:T(8,128)(2,1)S(1)} custom-call(bf16[256,768]{1,0:T(8,128)(2,1)S(1)} %get-tuple-element.44.mix_ref, bf16[256,512]{1,0:T(8,128)(2,1)S(1)} %get-tuple-element.60.grad_ref, bf16[256,512]{1,0:T(8,128)(2,1)S(1)} %bitcast.3, f32[256,512]{1,0:T(8,128)S(1)} %get-tuple-element.51.entering, ...), custom_call_target="tpu_custom_call" | custom-call | flops 268435456 | bytes 4458496 | tf_op jit(solution)/shard_map/pallas_call | solution.py:34
  76.7 0.6 collective-permute-start.11
  77.2 1.3 %collective-permute-done.11.other = bf16[256,512]{1,0:T(8,128)(2,1)S(1)} collective-permute-done((bf16[256,512]{1,0:T(8,128)(2,1)S(1)}, bf16[256,512]{1,0:T(8,128)(2,1)S(1)}, u32[]{:S(2)}, u32[]{:S(2)}) %collective-permute-start.11) | collective-permute-done | bytes 262176 | tf_op jit(solution)/shard_map/ppermute | solution.py:47
  79.1 0.6 shard_map.105
  79.7 1.7 %collective-permute-start.17 = (bf16[256,512]{1,0:T(8,128)(2,1)S(1)}, bf16[256,512]{1,0:T(8,128)(2,1)S(1)}, u32[]{:S(2)}, u32[]{:S(2)}) collective-permute-start(bf16[256,512]{1,0:T(8,128)(2,1)S(1)} %shard_map.105), channel_id=1, source_target_pairs={{0,2},{1,7},{2,4},{3,1},{4,6},{5,3},{6,0},{7,5},{8,10},{9,15},{10,... | collective-permute-start | bytes 786440 | tf_op jit(solution)/shard_map/ppermute | solution.py:56
  81.8 1.7 %collective-permute-start.12 = (bf16[256,512]{1,0:T(8,128)(2,1)S(1)}, bf16[256,512]{1,0:T(8,128)(2,1)S(1)}, u32[]{:S(2)}, u32[]{:S(2)}) collective-permute-start(bf16[256,512]{1,0:T(8,128)(2,1)S(1)} %shard_map.98), channel_id=1, source_target_pairs={{0,6},{1,3},{2,0},{3,5},{4,2},{5,7},{6,4},{7,1},{8,14},{9,11},{10,... | collective-permute-start | bytes 786440 | tf_op jit(solution)/shard_map/ppermute | solution.py:56
  83.5 0.7 shard_map.97
  84.2 0.6 shard_map.104
  84.8 2.1 %collective-permute-start.16 = (bf16[256,512]{1,0:T(8,128)(2,1)S(1)}, bf16[256,512]{1,0:T(8,128)(2,1)S(1)}, u32[]{:S(2)}, u32[]{:S(2)}) collective-permute-start(bf16[256,512]{1,0:T(8,128)(2,1)S(1)} %shard_map.104), channel_id=1, source_target_pairs={{0,6},{1,3},{2,0},{3,5},{4,2},{5,7},{6,4},{7,1},{8,14},{9,11},{10,... | collective-permute-start | bytes 786440 | tf_op jit(solution)/shard_map/ppermute | solution.py:56
  86.9 1.0 shard_map.103
  88.1 4.8 %collective-permute-done.17.refs_1_ = bf16[256,512]{1,0:T(8,128)(2,1)S(1)} collective-permute-done((bf16[256,512]{1,0:T(8,128)(2,1)S(1)}, bf16[256,512]{1,0:T(8,128)(2,1)S(1)}, u32[]{:S(2)}, u32[]{:S(2)}) %collective-permute-start.17) | collective-permute-done | bytes 262176 | tf_op jit(solution)/shard_map/ppermute | solution.py:56
  93.0 4.9 %collective-permute-done.14.refs_2_ = bf16[256,512]{1,0:T(8,128)(2,1)S(1)} collective-permute-done((bf16[256,512]{1,0:T(8,128)(2,1)S(1)}, bf16[256,512]{1,0:T(8,128)(2,1)S(1)}, u32[]{:S(2)}, u32[]{:S(2)}) %collective-permute-start.14) | collective-permute-done | bytes 262176 | tf_op jit(solution)/shard_map/ppermute | solution.py:56
  97.9 0.8 shard_map.101
  98.6 2.0 %collective-permute-done.18.refs_2_ = bf16[256,512]{1,0:T(8,128)(2,1)S(1)} collective-permute-done((bf16[256,512]{1,0:T(8,128)(2,1)S(1)}, bf16[256,512]{1,0:T(8,128)(2,1)S(1)}, u32[]{:S(2)}, u32[]{:S(2)}) %collective-permute-start.18) | collective-permute-done | bytes 262176 | tf_op jit(solution)/shard_map/ppermute | solution.py:56
  100.7 0.8 shard_map.107
  (38 shorter events, 3.5 us)
Async XLA Ops:
  0.6 3.4 %copy-start = (bf16[256,512]{1,0:T(8,128)(2,1)S(1)}, bf16[256,512]{1,0:T(8,128)(2,1)}, u32[]{:S(2)}) copy-start(bf16[256,512]{1,0:T(8,128)(2,1)} %own.2) | copy-start | bytes 786436
  0.6 13.3 %copy-start.1 = (bf16[256,512]{1,0:T(8,128)(2,1)S(1)}, bf16[256,512]{1,0:T(8,128)(2,1)}, u32[]{:S(2)}) copy-start(bf16[256,512]{1,0:T(8,128)(2,1)} %own.3) | copy-start | bytes 786436
  3.3 24.3 %collective-permute-start.2 = (bf16[4,512,512]{2,1,0:T(8,128)(2,1)S(1)}, bf16[4,512,512]{2,1,0:T(8,128)(2,1)S(1)}, u32[]{:S(2)}, u32[]{:S(2)}) collective-permute-start(bf16[4,512,512]{2,1,0:T(8,128)(2,1)S(1)} %get-tuple-element.35), channel_id=1, source_target_pairs={{0,1},{1,0},{2,3},{3,2},{4,5},{5,4},{6,7},{7,6},{8,9},{9,8},{10,11... | collective-permute-start | bytes 6291464 | tf_op jit(solution)/shard_map/ppermute | solution.py:47
  3.4 26.6 %collective-permute-start.8 = (bf16[4,512,512]{2,1,0:T(8,128)(2,1)S(1)}, bf16[4,512,512]{2,1,0:T(8,128)(2,1)S(1)}, u32[]{:S(2)}, u32[]{:S(2)}) collective-permute-start(bf16[4,512,512]{2,1,0:T(8,128)(2,1)S(1)} %get-tuple-element.46), channel_id=1, source_target_pairs={{0,1},{1,0},{2,3},{3,2},{4,5},{5,4},{6,7},{7,6},{8,9},{9,8},{10,11... | collective-permute-start | bytes 6291464 | tf_op jit(solution)/shard_map/ppermute | solution.py:47
  3.9 18.1 %collective-permute-start.3 = (bf16[4,512,256]{2,1,0:T(8,128)(2,1)S(1)}, bf16[4,512,256]{2,1,0:T(8,128)(2,1)S(1)}, u32[]{:S(2)}, u32[]{:S(2)}) collective-permute-start(bf16[4,512,256]{2,1,0:T(8,128)(2,1)S(1)} %get-tuple-element.36), channel_id=1, source_target_pairs={{0,1},{1,0},{2,3},{3,2},{4,5},{5,4},{6,7},{7,6},{8,9},{9,8},{10,11... | collective-permute-start | bytes 3145736 | tf_op jit(solution)/shard_map/ppermute | solution.py:47
  4.0 9.9 %collective-permute-start = (bf16[256,512]{1,0:T(8,128)(2,1)S(1)}, bf16[256,512]{1,0:T(8,128)(2,1)S(1)}, u32[]{:S(2)}, u32[]{:S(2)}) collective-permute-start(bf16[256,512]{1,0:T(8,128)(2,1)S(1)} %copy-done), channel_id=1, source_target_pairs={{0,2},{2,4},{4,6},{6,0},{1,3},{3,5},{5,7},{7,1},{8,10},{10,12},{12... | collective-permute-start | bytes 786440 | tf_op jit(solution)/shard_map/ppermute | solution.py:47
  5.6 10.1 %collective-permute-start.4 = (bf16[256,512]{1,0:T(8,128)(2,1)S(1)}, bf16[256,512]{1,0:T(8,128)(2,1)S(1)}, u32[]{:S(2)}, u32[]{:S(2)}) collective-permute-start(bf16[256,512]{1,0:T(8,128)(2,1)S(1)} %copy-done), channel_id=1, source_target_pairs={{0,6},{2,0},{4,2},{6,4},{1,7},{3,1},{5,3},{7,5},{8,14},{10,8},{12,... | collective-permute-start | bytes 786440 | tf_op jit(solution)/shard_map/ppermute | solution.py:47
  13.9 7.8 %collective-permute-start.6 = (bf16[256,512]{1,0:T(8,128)(2,1)S(1)}, bf16[256,512]{1,0:T(8,128)(2,1)S(1)}, u32[]{:S(2)}, u32[]{:S(2)}) collective-permute-start(bf16[256,512]{1,0:T(8,128)(2,1)S(1)} %copy-done.1), channel_id=1, source_target_pairs={{0,6},{2,0},{4,2},{6,4},{1,7},{3,1},{5,3},{7,5},{8,14},{10,8},{12,... | collective-permute-start | bytes 786440 | tf_op jit(solution)/shard_map/ppermute | solution.py:47
  15.6 13.3 %collective-permute-start.1 = (bf16[256,512]{1,0:T(8,128)(2,1)S(1)}, bf16[256,512]{1,0:T(8,128)(2,1)S(1)}, u32[]{:S(2)}, u32[]{:S(2)}) collective-permute-start(bf16[256,512]{1,0:T(8,128)(2,1)S(1)} %collective-permute-done.low), channel_id=1, source_target_pairs={{0,2},{2,4},{4,6},{6,0},{1,3},{3,5},{5,7},{7,1},{8,10},{10,12},{12... | collective-permute-start | bytes 786440 | tf_op jit(solution)/shard_map/ppermute | solution.py:47
  21.7 8.2 %collective-permute-start.9 = (bf16[256,512]{1,0:T(8,128)(2,1)S(1)}, bf16[256,512]{1,0:T(8,128)(2,1)S(1)}, u32[]{:S(2)}, u32[]{:S(2)}) collective-permute-start(bf16[256,512]{1,0:T(8,128)(2,1)S(1)} %copy-done.1), channel_id=1, source_target_pairs={{0,2},{2,4},{4,6},{6,0},{1,3},{3,5},{5,7},{7,1},{8,10},{10,12},{12... | collective-permute-start | bytes 786440 | tf_op jit(solution)/shard_map/ppermute | solution.py:47
  22.0 9.0 %collective-permute-start.7 = (bf16[256,512]{1,0:T(8,128)(2,1)S(1)}, bf16[256,512]{1,0:T(8,128)(2,1)S(1)}, u32[]{:S(2)}, u32[]{:S(2)}) collective-permute-start(bf16[256,512]{1,0:T(8,128)(2,1)S(1)} %collective-permute-done.6.high), channel_id=1, source_target_pairs={{0,6},{2,0},{4,2},{6,4},{1,7},{3,1},{5,3},{7,5},{8,14},{10,8},{12,... | collective-permute-start | bytes 786440 | tf_op jit(solution)/shard_map/ppermute | solution.py:47
  29.5 3.6 %collective-permute-start.5 = (bf16[256,768]{1,0:T(8,128)(2,1)S(1)}, bf16[256,768]{1,0:T(8,128)(2,1)S(1)}, u32[]{:S(2)}, u32[]{:S(2)}) collective-permute-start(bf16[256,768]{1,0:T(8,128)(2,1)S(1)} %get-tuple-element.40), channel_id=1, source_target_pairs={{0,1},{1,0},{2,3},{3,2},{4,5},{5,4},{6,7},{7,6},{8,9},{9,8},{10,11... | collective-permute-start | bytes 1179656 | tf_op jit(solution)/shard_map/ppermute | solution.py:47
  31.0 0.8 copy-start.2
  31.0 0.8 copy-start.3
  31.5 2.3 %collective-permute-start.10 = (bf16[256,512]{1,0:T(8,128)(2,1)S(1)}, bf16[256,512]{1,0:T(8,128)(2,1)S(1)}, u32[]{:S(2)}, u32[]{:S(2)}) collective-permute-start(bf16[256,512]{1,0:T(8,128)(2,1)S(1)} %get-tuple-element.50), channel_id=1, source_target_pairs={{0,1},{1,0},{2,3},{3,2},{4,5},{5,4},{6,7},{7,6},{8,9},{9,8},{10,11... | collective-permute-start | bytes 786440 | tf_op jit(solution)/shard_map/ppermute | solution.py:47
  76.3 2.7 %collective-permute-start.15 = (bf16[256,768]{1,0:T(8,128)(2,1)S(1)}, bf16[256,768]{1,0:T(8,128)(2,1)S(1)}, u32[]{:S(2)}, u32[]{:S(2)}) collective-permute-start(bf16[256,768]{1,0:T(8,128)(2,1)S(1)} %shard_map.102.fin), channel_id=1, source_target_pairs={{0,1},{1,0},{2,3},{3,2},{4,5},{5,4},{6,7},{7,6},{8,9},{9,8},{10,11... | collective-permute-start | bytes 1179656 | tf_op jit(solution)/shard_map/ppermute | solution.py:47
  76.7 1.9 %collective-permute-start.11 = (bf16[256,512]{1,0:T(8,128)(2,1)S(1)}, bf16[256,512]{1,0:T(8,128)(2,1)S(1)}, u32[]{:S(2)}, u32[]{:S(2)}) collective-permute-start(bf16[256,512]{1,0:T(8,128)(2,1)S(1)} %shard_map.96.fin), channel_id=1, source_target_pairs={{0,1},{1,0},{2,3},{3,2},{4,5},{5,4},{6,7},{7,6},{8,9},{9,8},{10,11... | collective-permute-start | bytes 786440 | tf_op jit(solution)/shard_map/ppermute | solution.py:47
  79.0 9.0 %collective-permute-start.13 = (bf16[256,512]{1,0:T(8,128)(2,1)S(1)}, bf16[256,512]{1,0:T(8,128)(2,1)S(1)}, u32[]{:S(2)}, u32[]{:S(2)}) collective-permute-start(bf16[256,512]{1,0:T(8,128)(2,1)S(1)} %shard_map.99), channel_id=1, source_target_pairs={{0,2},{1,7},{2,4},{3,1},{4,6},{5,3},{6,0},{7,5},{8,10},{9,15},{10,... | collective-permute-start | bytes 786440 | tf_op jit(solution)/shard_map/ppermute | solution.py:56
  79.7 13.2 %collective-permute-start.17 = (bf16[256,512]{1,0:T(8,128)(2,1)S(1)}, bf16[256,512]{1,0:T(8,128)(2,1)S(1)}, u32[]{:S(2)}, u32[]{:S(2)}) collective-permute-start(bf16[256,512]{1,0:T(8,128)(2,1)S(1)} %shard_map.105), channel_id=1, source_target_pairs={{0,2},{1,7},{2,4},{3,1},{4,6},{5,3},{6,0},{7,5},{8,10},{9,15},{10,... | collective-permute-start | bytes 786440 | tf_op jit(solution)/shard_map/ppermute | solution.py:56
  81.8 11.2 %collective-permute-start.12 = (bf16[256,512]{1,0:T(8,128)(2,1)S(1)}, bf16[256,512]{1,0:T(8,128)(2,1)S(1)}, u32[]{:S(2)}, u32[]{:S(2)}) collective-permute-start(bf16[256,512]{1,0:T(8,128)(2,1)S(1)} %shard_map.98), channel_id=1, source_target_pairs={{0,6},{1,3},{2,0},{3,5},{4,2},{5,7},{6,4},{7,1},{8,14},{9,11},{10,... | collective-permute-start | bytes 786440 | tf_op jit(solution)/shard_map/ppermute | solution.py:56
  84.8 13.8 %collective-permute-start.16 = (bf16[256,512]{1,0:T(8,128)(2,1)S(1)}, bf16[256,512]{1,0:T(8,128)(2,1)S(1)}, u32[]{:S(2)}, u32[]{:S(2)}) collective-permute-start(bf16[256,512]{1,0:T(8,128)(2,1)S(1)} %shard_map.104), channel_id=1, source_target_pairs={{0,6},{1,3},{2,0},{3,5},{4,2},{5,7},{6,4},{7,1},{8,14},{9,11},{10,... | collective-permute-start | bytes 786440 | tf_op jit(solution)/shard_map/ppermute | solution.py:56
  88.0 9.9 %collective-permute-start.14 = (bf16[256,512]{1,0:T(8,128)(2,1)S(1)}, bf16[256,512]{1,0:T(8,128)(2,1)S(1)}, u32[]{:S(2)}, u32[]{:S(2)}) collective-permute-start(bf16[256,512]{1,0:T(8,128)(2,1)S(1)} %shard_map.100), channel_id=1, source_target_pairs={{0,2},{1,7},{2,4},{3,1},{4,6},{5,3},{6,0},{7,5},{8,10},{9,15},{10,... | collective-permute-start | bytes 786440 | tf_op jit(solution)/shard_map/ppermute | solution.py:56
  92.9 7.8 %collective-permute-start.18 = (bf16[256,512]{1,0:T(8,128)(2,1)S(1)}, bf16[256,512]{1,0:T(8,128)(2,1)S(1)}, u32[]{:S(2)}, u32[]{:S(2)}) collective-permute-start(bf16[256,512]{1,0:T(8,128)(2,1)S(1)} %shard_map.106), channel_id=1, source_target_pairs={{0,2},{1,7},{2,4},{3,1},{4,6},{5,3},{6,0},{7,5},{8,10},{9,15},{10,... | collective-permute-start | bytes 786440 | tf_op jit(solution)/shard_map/ppermute | solution.py:56

commit v2 on v1

--- a/solution.py
+++ b/solution.py
@@ -274,20 +274,29 @@
     reader = mix_ref[:, width + STATE :]
     incoming = states_ref[:STATE, :]
     outgoing = states_ref[STATE:, :]
-    score_grad = jnp.zeros((rows, rows), F32)
+    half = rows // 2
+    upper = jnp.zeros((half, half), F32)
+    lower = jnp.zeros((half, rows), F32)
     for two in range(HEADS // 2):
         at = slice(two * 128, two * 128 + 128)
         value_pair = mix_ref[:, at]
         grad_pair = grad_ref[:, at]
         back = grad_pair.astype(F32) * skip_ref[:, at]
         back = back + dot(writer, outgoing[:, at], NN) * to_end[:, at]
+        early, late = back[:half], back[half:]
         for odd in range(2):
             h = 2 * two + odd
             grad_one = masked(grad_pair, odd)
-            back = back + dot(weight_ref[h], grad_one, TN)
-            score_grad = score_grad + dot(grad_one, value_pair, NT) * decay_ref[h].astype(F32)
-        out_ref[:, at] = back.astype(BF16)
-    score_grad = score_grad.astype(BF16)
+            early = early + dot(weight_ref[h, :, :half], grad_one, TN)
+            late = late + dot(weight_ref[h, half:, half:], grad_one[half:], TN)
+            kernel = decay_ref[h, :half, :half].astype(F32)
+            upper = upper + dot(grad_one[:half], value_pair[:half], NT) * kernel
+            kernel = decay_ref[h, half:, :].astype(F32)
+            lower = lower + dot(grad_one[half:], value_pair, NT) * kernel
+        out_ref[:half, at] = early.astype(BF16)
+        out_ref[half:, at] = late.astype(BF16)
+    upper = jnp.concatenate([upper, jnp.zeros((half, half), F32)], axis=1)
+    score_grad = jnp.concatenate([upper, lower], axis=0).astype(BF16)
     value_scaled = (mix_ref[:, :width].astype(F32) * to_end[...]).astype(BF16)
     write = dot(score_grad, reader, TN) + dot(value_scaled, outgoing, NT)
     out_ref[:, width : width + STATE] = write.astype(BF16)

time: 102 us -> 102 us (level)
  no operation moved by 1% of the time
where the time goes in v2:
time: 102 us; the launch traced here: 101 us
  blocking collectives  40.9 us (40%)
  waiting for transfers between devices  25.7 us (25%)
  Pallas kernels  17.9 us (18%)
  starting transfers between devices  16 us (16%)
    all_to_all x1, blocking collectives, per_device(): lax.all_to_all(pay.reshape(32, 8, width + 128), SEQ, 0, 0, tiled=True)  23.8 us
    all_to_all x1, blocking collectives, per_device(): lax.all_to_all(owned, SEQ, 0, 0, tiled=True).reshape(2 * STATE, width)  17.1 us
    ppermute x13, waiting for transfers between devices, shift(): lax.ppermute(array, axis, [(i, (i + step) % size) for i in range(size)])  14.1 us
    pallas_call x20, Pallas kernels, call(): pl.pallas_call(body, out_shape=outs, in_specs=[vmem] * len(args), out_spe...  12.7 us
    ppermute x6, waiting for transfers between devices, ring(): return lax.ppermute(array, ('y', 'c'), pairs)  11.6 us
    ppermute x13, starting transfers between devices, shift(): lax.ppermute(array, axis, [(i, (i + step) % size) for i in range(size)])  10.2 us
    ppermute x6, starting transfers between devices, ring(): return lax.ppermute(array, ('y', 'c'), pairs)  5.74 us
    pallas_call x2, Pallas kernels, weights_of(): pl.pallas_call(functools.partial(weights_kernel, other), out_shape=[spec(...  5.22 us
  transfers between devices with their start and end apart: 19, of which 7 were waited for; matrix products, arithmetic and copies ran while one was open for 0% of the time, Pallas kernels for 13%

profile of v2, /device:TPU:2, one launch (start us, length us, event | category | flops | bytes accessed | tf_op | source)
XLA Modules:
  0.0 101.4 jit_solution(17196334175289562875)
XLA Ops:
  0.6 2.6 %shard_map.87 = (bf16[4,512,512]{2,1,0:T(8,128)(2,1)S(1)}, bf16[4,512,256]{2,1,0:T(8,128)(2,1)S(1)}, bf16[4,512,512]{2,1,0:T(8,128)(2,1)S(1)}) custom-call(bf16[4096,512]{1,0:T(8,128)(2,1)} %value_ref.3, bf16[4096,256]{1,0:T(8,128)(2,1)} %state_ref.3, bf16[512,4096]{1,0:T(8,128)(2,1)} %out_ref.3), custom_call_target="tpu_custom_call" | custom-call | bytes 10485760 | tf_op jit(solution)/shard_map/pallas_call | solution.py:149
  3.4 0.5 collective-permute-start.8
  4.0 1.6 %collective-permute-start = (bf16[256,512]{1,0:T(8,128)(2,1)S(1)}, bf16[256,512]{1,0:T(8,128)(2,1)S(1)}, u32[]{:S(2)}, u32[]{:S(2)}) collective-permute-start(bf16[256,512]{1,0:T(8,128)(2,1)S(1)} %copy-done), channel_id=1, source_target_pairs={{0,2},{2,4},{4,6},{6,0},{1,3},{3,5},{5,7},{7,1},{8,10},{10,12},{12... | collective-permute-start | bytes 786440 | tf_op jit(solution)/shard_map/ppermute | solution.py:47
  5.6 1.7 %collective-permute-start.4 = (bf16[256,512]{1,0:T(8,128)(2,1)S(1)}, bf16[256,512]{1,0:T(8,128)(2,1)S(1)}, u32[]{:S(2)}, u32[]{:S(2)}) collective-permute-start(bf16[256,512]{1,0:T(8,128)(2,1)S(1)} %copy-done), channel_id=1, source_target_pairs={{0,6},{2,0},{4,2},{6,4},{1,7},{3,1},{5,3},{7,5},{8,14},{10,8},{12,... | collective-permute-start | bytes 786440 | tf_op jit(solution)/shard_map/ppermute | solution.py:47
  7.2 6.7 %collective-permute-done.low = bf16[256,512]{1,0:T(8,128)(2,1)S(1)} collective-permute-done((bf16[256,512]{1,0:T(8,128)(2,1)S(1)}, bf16[256,512]{1,0:T(8,128)(2,1)S(1)}, u32[]{:S(2)}, u32[]{:S(2)}) %collective-permute-start) | collective-permute-done | bytes 262176 | tf_op jit(solution)/shard_map/ppermute | solution.py:47
  13.9 1.7 %collective-permute-start.6 = (bf16[256,512]{1,0:T(8,128)(2,1)S(1)}, bf16[256,512]{1,0:T(8,128)(2,1)S(1)}, u32[]{:S(2)}, u32[]{:S(2)}) collective-permute-start(bf16[256,512]{1,0:T(8,128)(2,1)S(1)} %copy-done.1), channel_id=1, source_target_pairs={{0,6},{2,0},{4,2},{6,4},{1,7},{3,1},{5,3},{7,5},{8,14},{10,8},{12,... | collective-permute-start | bytes 786440 | tf_op jit(solution)/shard_map/ppermute | solution.py:47
  15.9 5.8 %collective-permute-done.6.high = bf16[256,512]{1,0:T(8,128)(2,1)S(1)} collective-permute-done((bf16[256,512]{1,0:T(8,128)(2,1)S(1)}, bf16[256,512]{1,0:T(8,128)(2,1)S(1)}, u32[]{:S(2)}, u32[]{:S(2)}) %collective-permute-start.6) | collective-permute-done | bytes 262176 | tf_op jit(solution)/shard_map/ppermute | solution.py:47
  22.0 3.0 %collective-permute-start.7 = (bf16[256,512]{1,0:T(8,128)(2,1)S(1)}, bf16[256,512]{1,0:T(8,128)(2,1)S(1)}, u32[]{:S(2)}, u32[]{:S(2)}) collective-permute-start(bf16[256,512]{1,0:T(8,128)(2,1)S(1)} %collective-permute-done.6.high), channel_id=1, source_target_pairs={{0,6},{2,0},{4,2},{6,4},{1,7},{3,1},{5,3},{7,5},{8,14},{10,8},{12,... | collective-permute-start | bytes 786440 | tf_op jit(solution)/shard_map/ppermute | solution.py:47
  25.0 2.6 %shard_map.86 = (bf16[4,512,512]{2,1,0:T(8,128)(2,1)S(1)}, bf16[4,512,256]{2,1,0:T(8,128)(2,1)S(1)}, bf16[4,512,512]{2,1,0:T(8,128)(2,1)S(1)}) custom-call(bf16[4096,512]{1,0:T(8,128)(2,1)} %value_ref.3, bf16[4096,256]{1,0:T(8,128)(2,1)} %state_ref.3, bf16[512,4096]{1,0:T(8,128)(2,1)} %out_ref.3), custom_call_target="tpu_custom_call" | custom-call | bytes 10485760 | tf_op jit(solution)/shard_map/pallas_call | solution.py:149
  27.6 1.4 %shard_map.88 = (f32[256,768]{1,0:T(8,128)S(1)}, f32[256,768]{1,0:T(8,128)S(1)}) custom-call(bf16[256,512]{1,0:T(8,128)(2,1)S(1)} %copy-done, bf16[256,512]{1,0:T(8,128)(2,1)S(1)} %collective-permute-done.low, bf16[256,512]{1,0:T(8,128)(2,1)S(1)} %collective-permute-done.4.high, bf16[4,512,512]{2,1,0:T(8,128)(2,1)S(1)} %get-tuple-element.33.value_a, ...), custom_call_target="tpu_custom_call" | custom-call | flops 1073741824 | bytes 8650752 | tf_op jit(solution)/shard_map/pallas_call | solution.py:34
  29.0 0.6 shard_map.89
  30.0 1.0 shard_map.92
  31.0 0.5 shard_map.93
  31.8 1.4 %shard_map.90 = (bf16[8,256,256]{2,1,0:T(8,128)(2,1)S(1)}, f32[256,512]{1,0:T(8,128)S(1)}, f32[256,512]{1,0:T(8,128)S(1)}, bf16[8,128]{1,0:T(8,128)(2,1)S(1)}, f32[1,512]{1,0:T(1,128)S(1)}) custom-call(f32[8,256]{1,0:T(8,128)S(1)} %copy-done.2, f32[1,8]{1,0:T(1,128)S(1)} %bitcast.6), custom_call_target="tpu_custom_call" | custom-call | flops 16777216 | bytes 2109472 | tf_op jit(solution)/shard_map/pallas_call | solution.py:34
  33.2 0.6 shard_map.91
  34.1 23.8 %all_to_all.10.pieces_ref = bf16[32,8,640]{2,1,0:T(8,128)(2,1)S(1)} all-to-all(bf16[32,8,640]{2,1,0:T(8,128)(2,1)S(1)} %bitcast.5), channel_id=1, replica_groups=mesh['x'=4,'z'=8,'y'=4,'c'=2] {'x','z'}, dimensions={0} | all-to-all | bytes 655360 | tf_op jit(solution)/shard_map/all_to_all | solution.py:408
  58.1 17.1 %all_to_all.11 = bf16[32,8,512]{2,1,0:T(8,128)(2,1)S(1)} all-to-all(bf16[32,8,512]{2,1,0:T(8,128)(2,1)S(1)} %shard_map.95), channel_id=1, replica_groups=mesh['x'=4,'z'=8,'y'=4,'c'=2] {'x','z'}, dimensions={0} | all-to-all | bytes 524288 | tf_op jit(solution)/shard_map/all_to_all | solution.py:412
  75.2 1.1 %shard_map.102.fin = bf16[256,768]{1,0:T(8,128)(2,1)S(1)} custom-call(bf16[256,768]{1,0:T(8,128)(2,1)S(1)} %get-tuple-element.44.mix_ref, bf16[256,512]{1,0:T(8,128)(2,1)S(1)} %get-tuple-element.60.grad_ref, bf16[256,512]{1,0:T(8,128)(2,1)S(1)} %bitcast.3, f32[256,512]{1,0:T(8,128)S(1)} %get-tuple-element.51.entering, ...), custom_call_target="tpu_custom_call" | custom-call | flops 268435456 | bytes 4458496 | tf_op jit(solution)/shard_map/pallas_call | solution.py:34
  76.6 0.6 collective-permute-start.11
  77.2 1.3 %collective-permute-done.11.other = bf16[256,512]{1,0:T(8,128)(2,1)S(1)} collective-permute-done((bf16[256,512]{1,0:T(8,128)(2,1)S(1)}, bf16[256,512]{1,0:T(8,128)(2,1)S(1)}, u32[]{:S(2)}, u32[]{:S(2)}) %collective-permute-start.11) | collective-permute-done | bytes 262176 | tf_op jit(solution)/shard_map/ppermute | solution.py:47
  79.0 0.6 shard_map.105
  79.7 1.7 %collective-permute-start.17 = (bf16[256,512]{1,0:T(8,128)(2,1)S(1)}, bf16[256,512]{1,0:T(8,128)(2,1)S(1)}, u32[]{:S(2)}, u32[]{:S(2)}) collective-permute-start(bf16[256,512]{1,0:T(8,128)(2,1)S(1)} %shard_map.105), channel_id=1, source_target_pairs={{0,2},{1,7},{2,4},{3,1},{4,6},{5,3},{6,0},{7,5},{8,10},{9,15},{10,... | collective-permute-start | bytes 786440 | tf_op jit(solution)/shard_map/ppermute | solution.py:56
  81.8 1.7 %collective-permute-start.12 = (bf16[256,512]{1,0:T(8,128)(2,1)S(1)}, bf16[256,512]{1,0:T(8,128)(2,1)S(1)}, u32[]{:S(2)}, u32[]{:S(2)}) collective-permute-start(bf16[256,512]{1,0:T(8,128)(2,1)S(1)} %shard_map.98), channel_id=1, source_target_pairs={{0,6},{1,3},{2,0},{3,5},{4,2},{5,7},{6,4},{7,1},{8,14},{9,11},{10,... | collective-permute-start | bytes 786440 | tf_op jit(solution)/shard_map/ppermute | solution.py:56
  83.5 0.7 shard_map.97
  84.2 0.6 shard_map.104
  84.8 2.1 %collective-permute-start.16 = (bf16[256,512]{1,0:T(8,128)(2,1)S(1)}, bf16[256,512]{1,0:T(8,128)(2,1)S(1)}, u32[]{:S(2)}, u32[]{:S(2)}) collective-permute-start(bf16[256,512]{1,0:T(8,128)(2,1)S(1)} %shard_map.104), channel_id=1, source_target_pairs={{0,6},{1,3},{2,0},{3,5},{4,2},{5,7},{6,4},{7,1},{8,14},{9,11},{10,... | collective-permute-start | bytes 786440 | tf_op jit(solution)/shard_map/ppermute | solution.py:56
  86.9 1.0 shard_map.103
  88.1 4.8 %collective-permute-done.17.refs_1_ = bf16[256,512]{1,0:T(8,128)(2,1)S(1)} collective-permute-done((bf16[256,512]{1,0:T(8,128)(2,1)S(1)}, bf16[256,512]{1,0:T(8,128)(2,1)S(1)}, u32[]{:S(2)}, u32[]{:S(2)}) %collective-permute-start.17) | collective-permute-done | bytes 262176 | tf_op jit(solution)/shard_map/ppermute | solution.py:56
  93.0 4.9 %collective-permute-done.14.refs_2_ = bf16[256,512]{1,0:T(8,128)(2,1)S(1)} collective-permute-done((bf16[256,512]{1,0:T(8,128)(2,1)S(1)}, bf16[256,512]{1,0:T(8,128)(2,1)S(1)}, u32[]{:S(2)}, u32[]{:S(2)}) %collective-permute-start.14) | collective-permute-done | bytes 262176 | tf_op jit(solution)/shard_map/ppermute | solution.py:56
  97.8 0.8 shard_map.101
  98.6 2.0 %collective-permute-done.18.refs_2_ = bf16[256,512]{1,0:T(8,128)(2,1)S(1)} collective-permute-done((bf16[256,512]{1,0:T(8,128)(2,1)S(1)}, bf16[256,512]{1,0:T(8,128)(2,1)S(1)}, u32[]{:S(2)}, u32[]{:S(2)}) %collective-permute-start.18) | collective-permute-done | bytes 262176 | tf_op jit(solution)/shard_map/ppermute | solution.py:56
  100.6 0.8 shard_map.107
  (38 shorter events, 3.5 us)
Async XLA Ops:
  0.6 3.4 %copy-start = (bf16[256,512]{1,0:T(8,128)(2,1)S(1)}, bf16[256,512]{1,0:T(8,128)(2,1)}, u32[]{:S(2)}) copy-start(bf16[256,512]{1,0:T(8,128)(2,1)} %own.2) | copy-start | bytes 786436
  0.6 13.3 %copy-start.1 = (bf16[256,512]{1,0:T(8,128)(2,1)S(1)}, bf16[256,512]{1,0:T(8,128)(2,1)}, u32[]{:S(2)}) copy-start(bf16[256,512]{1,0:T(8,128)(2,1)} %own.3) | copy-start | bytes 786436
  3.3 24.3 %collective-permute-start.2 = (bf16[4,512,512]{2,1,0:T(8,128)(2,1)S(1)}, bf16[4,512,512]{2,1,0:T(8,128)(2,1)S(1)}, u32[]{:S(2)}, u32[]{:S(2)}) collective-permute-start(bf16[4,512,512]{2,1,0:T(8,128)(2,1)S(1)} %get-tuple-element.35), channel_id=1, source_target_pairs={{0,1},{1,0},{2,3},{3,2},{4,5},{5,4},{6,7},{7,6},{8,9},{9,8},{10,11... | collective-permute-start | bytes 6291464 | tf_op jit(solution)/shard_map/ppermute | solution.py:47
  3.4 26.6 %collective-permute-start.8 = (bf16[4,512,512]{2,1,0:T(8,128)(2,1)S(1)}, bf16[4,512,512]{2,1,0:T(8,128)(2,1)S(1)}, u32[]{:S(2)}, u32[]{:S(2)}) collective-permute-start(bf16[4,512,512]{2,1,0:T(8,128)(2,1)S(1)} %get-tuple-element.46), channel_id=1, source_target_pairs={{0,1},{1,0},{2,3},{3,2},{4,5},{5,4},{6,7},{7,6},{8,9},{9,8},{10,11... | collective-permute-start | bytes 6291464 | tf_op jit(solution)/shard_map/ppermute | solution.py:47
  3.9 18.1 %collective-permute-start.3 = (bf16[4,512,256]{2,1,0:T(8,128)(2,1)S(1)}, bf16[4,512,256]{2,1,0:T(8,128)(2,1)S(1)}, u32[]{:S(2)}, u32[]{:S(2)}) collective-permute-start(bf16[4,512,256]{2,1,0:T(8,128)(2,1)S(1)} %get-tuple-element.36), channel_id=1, source_target_pairs={{0,1},{1,0},{2,3},{3,2},{4,5},{5,4},{6,7},{7,6},{8,9},{9,8},{10,11... | collective-permute-start | bytes 3145736 | tf_op jit(solution)/shard_map/ppermute | solution.py:47
  4.0 9.9 %collective-permute-start = (bf16[256,512]{1,0:T(8,128)(2,1)S(1)}, bf16[256,512]{1,0:T(8,128)(2,1)S(1)}, u32[]{:S(2)}, u32[]{:S(2)}) collective-permute-start(bf16[256,512]{1,0:T(8,128)(2,1)S(1)} %copy-done), channel_id=1, source_target_pairs={{0,2},{2,4},{4,6},{6,0},{1,3},{3,5},{5,7},{7,1},{8,10},{10,12},{12... | collective-permute-start | bytes 786440 | tf_op jit(solution)/shard_map/ppermute | solution.py:47
  5.6 10.1 %collective-permute-start.4 = (bf16[256,512]{1,0:T(8,128)(2,1)S(1)}, bf16[256,512]{1,0:T(8,128)(2,1)S(1)}, u32[]{:S(2)}, u32[]{:S(2)}) collective-permute-start(bf16[256,512]{1,0:T(8,128)(2,1)S(1)} %copy-done), channel_id=1, source_target_pairs={{0,6},{2,0},{4,2},{6,4},{1,7},{3,1},{5,3},{7,5},{8,14},{10,8},{12,... | collective-permute-start | bytes 786440 | tf_op jit(solution)/shard_map/ppermute | solution.py:47
  13.9 7.8 %collective-permute-start.6 = (bf16[256,512]{1,0:T(8,128)(2,1)S(1)}, bf16[256,512]{1,0:T(8,128)(2,1)S(1)}, u32[]{:S(2)}, u32[]{:S(2)}) collective-permute-start(bf16[256,512]{1,0:T(8,128)(2,1)S(1)} %copy-done.1), channel_id=1, source_target_pairs={{0,6},{2,0},{4,2},{6,4},{1,7},{3,1},{5,3},{7,5},{8,14},{10,8},{12,... | collective-permute-start | bytes 786440 | tf_op jit(solution)/shard_map/ppermute | solution.py:47
  15.6 13.3 %collective-permute-start.1 = (bf16[256,512]{1,0:T(8,128)(2,1)S(1)}, bf16[256,512]{1,0:T(8,128)(2,1)S(1)}, u32[]{:S(2)}, u32[]{:S(2)}) collective-permute-start(bf16[256,512]{1,0:T(8,128)(2,1)S(1)} %collective-permute-done.low), channel_id=1, source_target_pairs={{0,2},{2,4},{4,6},{6,0},{1,3},{3,5},{5,7},{7,1},{8,10},{10,12},{12... | collective-permute-start | bytes 786440 | tf_op jit(solution)/shard_map/ppermute | solution.py:47
  21.7 8.2 %collective-permute-start.9 = (bf16[256,512]{1,0:T(8,128)(2,1)S(1)}, bf16[256,512]{1,0:T(8,128)(2,1)S(1)}, u32[]{:S(2)}, u32[]{:S(2)}) collective-permute-start(bf16[256,512]{1,0:T(8,128)(2,1)S(1)} %copy-done.1), channel_id=1, source_target_pairs={{0,2},{2,4},{4,6},{6,0},{1,3},{3,5},{5,7},{7,1},{8,10},{10,12},{12... | collective-permute-start | bytes 786440 | tf_op jit(solution)/shard_map/ppermute | solution.py:47
  22.0 9.0 %collective-permute-start.7 = (bf16[256,512]{1,0:T(8,128)(2,1)S(1)}, bf16[256,512]{1,0:T(8,128)(2,1)S(1)}, u32[]{:S(2)}, u32[]{:S(2)}) collective-permute-start(bf16[256,512]{1,0:T(8,128)(2,1)S(1)} %collective-permute-done.6.high), channel_id=1, source_target_pairs={{0,6},{2,0},{4,2},{6,4},{1,7},{3,1},{5,3},{7,5},{8,14},{10,8},{12,... | collective-permute-start | bytes 786440 | tf_op jit(solution)/shard_map/ppermute | solution.py:47
  29.5 3.6 %collective-permute-start.5 = (bf16[256,768]{1,0:T(8,128)(2,1)S(1)}, bf16[256,768]{1,0:T(8,128)(2,1)S(1)}, u32[]{:S(2)}, u32[]{:S(2)}) collective-permute-start(bf16[256,768]{1,0:T(8,128)(2,1)S(1)} %get-tuple-element.40), channel_id=1, source_target_pairs={{0,1},{1,0},{2,3},{3,2},{4,5},{5,4},{6,7},{7,6},{8,9},{9,8},{10,11... | collective-permute-start | bytes 1179656 | tf_op jit(solution)/shard_map/ppermute | solution.py:47
  31.0 0.8 copy-start.2
  31.0 0.8 copy-start.3
  31.5 2.3 %collective-permute-start.10 = (bf16[256,512]{1,0:T(8,128)(2,1)S(1)}, bf16[256,512]{1,0:T(8,128)(2,1)S(1)}, u32[]{:S(2)}, u32[]{:S(2)}) collective-permute-start(bf16[256,512]{1,0:T(8,128)(2,1)S(1)} %get-tuple-element.50), channel_id=1, source_target_pairs={{0,1},{1,0},{2,3},{3,2},{4,5},{5,4},{6,7},{7,6},{8,9},{9,8},{10,11... | collective-permute-start | bytes 786440 | tf_op jit(solution)/shard_map/ppermute | solution.py:47
  76.3 2.7 %collective-permute-start.15 = (bf16[256,768]{1,0:T(8,128)(2,1)S(1)}, bf16[256,768]{1,0:T(8,128)(2,1)S(1)}, u32[]{:S(2)}, u32[]{:S(2)}) collective-permute-start(bf16[256,768]{1,0:T(8,128)(2,1)S(1)} %shard_map.102.fin), channel_id=1, source_target_pairs={{0,1},{1,0},{2,3},{3,2},{4,5},{5,4},{6,7},{7,6},{8,9},{9,8},{10,11... | collective-permute-start | bytes 1179656 | tf_op jit(solution)/shard_map/ppermute | solution.py:47
  76.6 1.9 %collective-permute-start.11 = (bf16[256,512]{1,0:T(8,128)(2,1)S(1)}, bf16[256,512]{1,0:T(8,128)(2,1)S(1)}, u32[]{:S(2)}, u32[]{:S(2)}) collective-permute-start(bf16[256,512]{1,0:T(8,128)(2,1)S(1)} %shard_map.96.fin), channel_id=1, source_target_pairs={{0,1},{1,0},{2,3},{3,2},{4,5},{5,4},{6,7},{7,6},{8,9},{9,8},{10,11... | collective-permute-start | bytes 786440 | tf_op jit(solution)/shard_map/ppermute | solution.py:47
  78.9 9.0 %collective-permute-start.13 = (bf16[256,512]{1,0:T(8,128)(2,1)S(1)}, bf16[256,512]{1,0:T(8,128)(2,1)S(1)}, u32[]{:S(2)}, u32[]{:S(2)}) collective-permute-start(bf16[256,512]{1,0:T(8,128)(2,1)S(1)} %shard_map.99), channel_id=1, source_target_pairs={{0,2},{1,7},{2,4},{3,1},{4,6},{5,3},{6,0},{7,5},{8,10},{9,15},{10,... | collective-permute-start | bytes 786440 | tf_op jit(solution)/shard_map/ppermute | solution.py:56
  79.7 13.2 %collective-permute-start.17 = (bf16[256,512]{1,0:T(8,128)(2,1)S(1)}, bf16[256,512]{1,0:T(8,128)(2,1)S(1)}, u32[]{:S(2)}, u32[]{:S(2)}) collective-permute-start(bf16[256,512]{1,0:T(8,128)(2,1)S(1)} %shard_map.105), channel_id=1, source_target_pairs={{0,2},{1,7},{2,4},{3,1},{4,6},{5,3},{6,0},{7,5},{8,10},{9,15},{10,... | collective-permute-start | bytes 786440 | tf_op jit(solution)/shard_map/ppermute | solution.py:56
  81.8 11.2 %collective-permute-start.12 = (bf16[256,512]{1,0:T(8,128)(2,1)S(1)}, bf16[256,512]{1,0:T(8,128)(2,1)S(1)}, u32[]{:S(2)}, u32[]{:S(2)}) collective-permute-start(bf16[256,512]{1,0:T(8,128)(2,1)S(1)} %shard_map.98), channel_id=1, source_target_pairs={{0,6},{1,3},{2,0},{3,5},{4,2},{5,7},{6,4},{7,1},{8,14},{9,11},{10,... | collective-permute-start | bytes 786440 | tf_op jit(solution)/shard_map/ppermute | solution.py:56
  84.8 13.8 %collective-permute-start.16 = (bf16[256,512]{1,0:T(8,128)(2,1)S(1)}, bf16[256,512]{1,0:T(8,128)(2,1)S(1)}, u32[]{:S(2)}, u32[]{:S(2)}) collective-permute-start(bf16[256,512]{1,0:T(8,128)(2,1)S(1)} %shard_map.104), channel_id=1, source_target_pairs={{0,6},{1,3},{2,0},{3,5},{4,2},{5,7},{6,4},{7,1},{8,14},{9,11},{10,... | collective-permute-start | bytes 786440 | tf_op jit(solution)/shard_map/ppermute | solution.py:56
  88.0 9.9 %collective-permute-start.14 = (bf16[256,512]{1,0:T(8,128)(2,1)S(1)}, bf16[256,512]{1,0:T(8,128)(2,1)S(1)}, u32[]{:S(2)}, u32[]{:S(2)}) collective-permute-start(bf16[256,512]{1,0:T(8,128)(2,1)S(1)} %shard_map.100), channel_id=1, source_target_pairs={{0,2},{1,7},{2,4},{3,1},{4,6},{5,3},{6,0},{7,5},{8,10},{9,15},{10,... | collective-permute-start | bytes 786440 | tf_op jit(solution)/shard_map/ppermute | solution.py:56
  92.9 7.8 %collective-permute-start.18 = (bf16[256,512]{1,0:T(8,128)(2,1)S(1)}, bf16[256,512]{1,0:T(8,128)(2,1)S(1)}, u32[]{:S(2)}, u32[]{:S(2)}) collective-permute-start(bf16[256,512]{1,0:T(8,128)(2,1)S(1)} %shard_map.106), channel_id=1, source_target_pairs={{0,2},{1,7},{2,4},{3,1},{4,6},{5,3},{6,0},{7,5},{8,10},{9,15},{10,... | collective-permute-start | bytes 786440 | tf_op jit(solution)/shard_map/ppermute | solution.py:56
